TPU v7x, 32 devices: a whole 2x2x4 slice. The times are simulated.
32 devices in a mesh: dp: 32 (over z, y, x, core).
Axes of the slice: x: 2, y: 2, z: 4, core: 2. Of those that a mesh axis runs over, the one named last changes fastest.
Arguments:
- tokens: bfloat16 [32768, 512], P('dp'), may hold values from -6 to 6
- timesteps: int32 [32], P('dp'), may hold values from 0 to 49
- w_qkv: bfloat16 [512, 1536], P('dp'), may hold values from -0.375 to 0.375
- w_out: bfloat16 [512, 512], P('dp'), may hold values from -1 to 1
- w_up: bfloat16 [512, 2048], P('dp'), may hold values from -0.25 to 0.25
- w_down: bfloat16 [2048, 512], P('dp'), may hold values from -0.1875 to 0.1875
- gain_attn: bfloat16 [512], P('dp'), may hold values from 0.25 to 1.75
- shift_attn: bfloat16 [512], P('dp'), may hold values from -1.75 to 1.75
- gain_ffn: bfloat16 [512], P('dp'), may hold values from 0.25 to 1.75
- shift_ffn: bfloat16 [512], P('dp'), may hold values from -1.75 to 1.75
- bias_query: bfloat16 [512], P('dp'), may hold values from -3 to 3
- bias_value: bfloat16 [512], P('dp'), may hold values from -3 to 3
- bias_out: bfloat16 [512], P('dp'), may hold values from -3 to 3
- bias_up: bfloat16 [2048], P('dp'), may hold values from -3 to 3
- bias_down: bfloat16 [512], P('dp'), may hold values from -3 to 3
- step_table: bfloat16 [50, 512], P(None, 'dp'), may hold values from -3 to 3
- cotangent: bfloat16 [32768, 512], P('dp'), may hold values from -6 to 6
Outputs:
- output: bfloat16 [32768, 512], P('dp')
- grad_tokens: float32 [32768, 512], P('dp')
- grad_w_qkv: float32 [512, 1536], P('dp')
- grad_w_out: float32 [512, 512], P('dp')
- grad_w_up: float32 [512, 2048], P('dp')
- grad_w_down: float32 [2048, 512], P('dp')
- grad_gain_attn: float32 [512], P('dp')
- grad_shift_attn: float32 [512], P('dp')
- grad_gain_ffn: float32 [512], P('dp')
- grad_shift_ffn: float32 [512], P('dp')
- grad_bias_query: float32 [512], P('dp')
- grad_bias_value: float32 [512], P('dp')
- grad_bias_out: float32 [512], P('dp')
- grad_bias_up: float32 [2048], P('dp')
- grad_bias_down: float32 [512], P('dp')
- grad_step_table: float32 [50, 512], P(None, 'dp')
All inputs are finite; a program needn't handle non-finite values.
Results may differ from a plain program's by a relative error of at most 0.014.
Values may be sent and summed in bfloat16 or wider, within the bound.
No kernel may reach another device: no remote copies, remote signals or barrier semaphores. Data moves between devices by JAX's collectives and lax.ppermute only.
A program may use at most 192 MiB of HBM per device.

v0:
```python
import functools
import jax
import jax.numpy as jnp
from jax import lax
from jax.experimental import pallas as pl
from jax.experimental.pallas import tpu as pltpu
from jax.sharding import PartitionSpec as P

HEAD_DIM = 64
PAIR = 2 * HEAD_DIM
EPSILON = 1e-05
SCALE_FACTOR = 0.125
BF16 = jnp.bfloat16
F32 = jnp.float32
NT = (((1,), (1,)), ((), ()))
TN = (((0,), (0,)), ((), ()))


def dot(left, right, dims=(((1,), (0,)), ((), ()))):
    return lax.dot_general(left, right, dims, preferred_element_type=F32)


def normalize(hidden):
    centred = hidden - jnp.mean(hidden, axis=-1, keepdims=True)
    inverse = lax.rsqrt(jnp.mean(centred * centred, axis=-1, keepdims=True) + EPSILON)
    return centred * inverse, inverse


def norm_back(grad_out, gain, normed, inverse):
    scaled = grad_out * gain
    return inverse * (
        scaled
        - jnp.mean(scaled, axis=-1, keepdims=True)
        - normed * jnp.mean(scaled * normed, axis=-1, keepdims=True)
    )


def whole(shape):
    zeros = (0,) * len(shape)
    return pl.BlockSpec(shape, lambda *_: zeros)


def call(kernel, grid, in_specs, out_specs, out_shape, flops, scratch=(), exps=0, name=None, aliases=None):
    moved = sum(s.size * s.dtype.itemsize for s in out_shape) * 2
    return pl.pallas_call(
        kernel,
        grid=grid,
        in_specs=in_specs,
        out_specs=out_specs,
        out_shape=out_shape,
        scratch_shapes=list(scratch),
        input_output_aliases=aliases or {},
        compiler_params=pltpu.CompilerParams(vmem_limit_bytes=56 * 1024 * 1024),
        cost_estimate=pl.CostEstimate(flops=flops, bytes_accessed=moved, transcendentals=exps),
        name=name,
    )


GAIN_A, SHIFT_A, GAIN_F, SHIFT_F, BIAS_Q, BIAS_V, BIAS_OUT, BIAS_DOWN = range(8)
LANES = 128
TILE = 16


def pack_kernel(w, table, *refs):
    vectors, up, out, held = refs[:8], refs[8], refs[9], refs[10]
    own, steps = table.shape
    cols = w.shape[1]
    held[...] = jnp.zeros_like(held)
    for k, vector in enumerate(vectors):
        held[64 + k : 65 + k, 0:own] = vector[...].astype(F32).reshape(1, own)
    wide = up[...].astype(F32).reshape(1, up.shape[0])
    for k in range(up.shape[0] // own):
        held[72 + k : 73 + k, 0:own] = wide[:, k * own : (k + 1) * own]
    packed = held[...].T[0:own, :].astype(BF16)
    out[:, 0:cols] = w[...]
    out[:, cols:] = packed
    out[:, cols : cols + steps] = table[...]


def pack(w, table, vectors, bias_up):
    own, cols = w.shape
    vmem = pl.BlockSpec(memory_space=pltpu.VMEM)
    return pl.pallas_call(
        pack_kernel,
        in_specs=[vmem] * 11,
        out_specs=vmem,
        out_shape=jax.ShapeDtypeStruct((own, cols + LANES), BF16),
        scratch_shapes=[pltpu.VMEM((LANES, LANES), F32)],
        name="pack",
    )(w, table.T, *vectors, bias_up)


def join_kernel(w_out, w_up, w_down, out):
    own, width = w_out.shape
    edge = width + w_up.shape[1]
    out[:, 0:width] = w_out[...]
    out[:, width:edge] = w_up[...]
    for fold in range(w_down.shape[0] // own):
        out[:, edge + fold * width : edge + (fold + 1) * width] = w_down[fold * own : (fold + 1) * own, :]


def join(w_out, w_up, w_down):
    own, width = w_out.shape
    columns = width + w_up.shape[1] + w_down.shape[0] // own * width
    vmem = pl.BlockSpec(memory_space=pltpu.VMEM)
    return pl.pallas_call(
        join_kernel,
        in_specs=[vmem] * 3,
        out_specs=vmem,
        out_shape=jax.ShapeDtypeStruct((own, columns), BF16),
        name="join",
    )(w_out, w_up, w_down)


def folded_place(own, folds, fold, shape, feature_axis):
    feature = lax.broadcasted_iota(jnp.int32, shape, feature_axis)
    unit = lax.broadcasted_iota(jnp.int32, shape, 1 - feature_axis)
    device = lax.div(feature, own)
    place = device * (own * folds) + fold * own + (feature - device * own)
    return jnp.where(unit == place, 1.0, 0.0).astype(BF16)


def split_two(value):
    high = value.astype(BF16)
    return high, (value - high.astype(F32)).astype(BF16)


def rows_at(block, fold=1):
    return pl.ds(pl.multiple_of(block * (TILE * fold), TILE * fold), TILE * fold)


def in_order(me, sources, apart, columns, target):
    for source, steps in zip(sources, apart):
        for block, step in enumerate(steps):
            target[rows_at(me ^ step), :] = source[block * TILE : (block + 1) * TILE, columns]


def project_kernel(apart, own, folds, me_ref, time_ref, tok, *refs):
    sources = refs[: len(apart)]
    proj_out, turned_out, w_out, vec, b_up, small, held = refs[len(apart) :]
    cols = w_out.shape[1]

    @pl.when(pl.program_id(0) == 0)
    def _():
        me = me_ref[0]
        in_order(me, sources, apart, slice(0, cols), w_out)
        in_order(me, sources, apart, slice(cols, cols + LANES), small)
        held[...] = small[...].astype(F32).T
        vec[0:8, :] = held[64:72, :]
        vec[8:9, :] = held[pl.ds(time_ref[0], 1), :]
        vec[9:16, :] = jnp.full((7, vec.shape[1]), time_ref[0].astype(F32))
        wide = jnp.zeros(b_up.shape, F32)
        for fold in range(folds):
            row = held[72 + fold : 73 + fold, :]
            rows = [row[:, at : at + LANES] for at in range(0, row.shape[1], LANES)]
            rows = jnp.concatenate(rows + rows, axis=0)[0:8].astype(BF16)
            wide = wide + dot(rows, folded_place(own, folds, fold, (LANES, LANES * folds), 0))
        b_up[...] = wide

    start = tok[...].astype(F32) + vec[8:9, :]
    normed, _ = normalize(start)
    entry = (normed * vec[GAIN_A : GAIN_A + 1, :] + vec[SHIFT_A : SHIFT_A + 1, :]).astype(BF16)
    turned_out[...] = entry.T
    product = dot(entry, w_out[...])
    width = tok.shape[1]
    proj_out[:, :width] = (product[:, :width] + vec[BIAS_Q : BIAS_Q + 1, :]).astype(BF16)
    proj_out[:, width : 2 * width] = product[:, width : 2 * width].astype(BF16)
    proj_out[:, 2 * width :] = (product[:, 2 * width :] + vec[BIAS_V : BIAS_V + 1, :]).astype(BF16)


def project(me, timesteps, tokens, sources, apart, own, folds, block=256):
    rows, width = tokens.shape
    cols = sources[0].shape[1] - LANES
    smem = pl.BlockSpec(memory_space=pltpu.SMEM)
    return call(
        functools.partial(project_kernel, apart, own, folds),
        (rows // block,),
        [
            smem,
            smem,
            pl.BlockSpec((block, width), lambda i: (i, 0)),
        ]
        + [whole(source.shape) for source in sources],
        [
            pl.BlockSpec((block, cols), lambda i: (i, 0)),
            pl.BlockSpec((width, block), lambda i: (0, i)),
            whole((width, cols)),
            whole((16, width)),
            whole((8, LANES * folds)),
        ],
        [
            jax.ShapeDtypeStruct((rows, cols), BF16),
            jax.ShapeDtypeStruct((width, rows), BF16),
            jax.ShapeDtypeStruct((width, cols), BF16),
            jax.ShapeDtypeStruct((16, width), F32),
            jax.ShapeDtypeStruct((8, LANES * folds), F32),
        ],
        2 * rows * width * cols,
        scratch=[pltpu.VMEM((width, LANES), BF16), pltpu.VMEM((LANES, width), F32)],
        name="project",
    )(me, timesteps, tokens, *sources)


def attend_kernel(block, q_ref, k_ref, v_ref, mixed_out, stat_out):
    rows = q_ref.shape[0]
    first = lax.broadcasted_iota(jnp.int32, (1, PAIR), 1) < HEAD_DIM
    keys_in = k_ref[...]
    values = jnp.concatenate([v_ref[...], jnp.ones((rows, PAIR), BF16)], axis=1)
    for at in range(0, rows, block):
        queries = q_ref[at : at + block, :] * BF16(SCALE_FACTOR)
        parts = []
        for head in range(2):
            own = first if head == 0 else jnp.logical_not(first)
            scores = dot(jnp.where(own, queries, BF16(0)), keys_in, NT)
            top = jnp.max(scores, axis=1, keepdims=True)
            raised = jnp.exp(scores - top).astype(BF16)
            both = dot(raised, values)
            total = both[:, PAIR:]
            parts.append((both[:, :PAIR] / total, top + jnp.log(total)))
        mixed_out[at : at + block, :] = jnp.where(first, parts[0][0], parts[1][0]).astype(BF16)
        stat_out[at : at + block, :] = jnp.where(first, parts[1][1], parts[0][1])


def attend(proj, block=256):
    rows, cols = proj.shape
    width = cols // 3
    pairs = width // PAIR
    return call(
        functools.partial(attend_kernel, block),
        (pairs,),
        [
            pl.BlockSpec((rows, PAIR), lambda p: (0, p)),
            pl.BlockSpec((rows, PAIR), lambda p: (0, pairs + p)),
            pl.BlockSpec((rows, PAIR), lambda p: (0, 2 * pairs + p)),
        ],
        [pl.BlockSpec((rows, PAIR), lambda p: (0, p))] * 2,
        [
            jax.ShapeDtypeStruct((rows, width), BF16),
            jax.ShapeDtypeStruct((rows, width), F32),
        ],
        4 * rows * rows * width,
        exps=rows * rows * width // HEAD_DIM,
        name="attend",
    )(proj, proj, proj)


def three_parts(value):
    high = value.astype(BF16).astype(F32)
    middle = (value - high).astype(BF16).astype(F32)
    return high, middle, value - high - middle


def attend_back_kernel(
    block, leaving, kept, me_ref, q_ref, k_ref, v_ref, g_ref, mixed_ref, stat_ref, turned_ref, *refs
):
    refs = refs[kept:]
    grad_out, sums_out = refs[:2]
    targets = refs[2 : 2 + len(leaving)]
    held = refs[-1]
    rows = q_ref.shape[0]
    lane = lax.broadcasted_iota(jnp.int32, (1, PAIR), 1)
    first = lane < HEAD_DIM
    spot = lax.rem(lane, HEAD_DIM)
    queries = q_ref[...] * BF16(SCALE_FACTOR)
    grads = g_ref[...]
    product = grads.astype(F32) * mixed_ref[...].astype(F32)
    logs = three_parts(stat_ref[...])
    minus = jnp.where(spot < 3, BF16(-1), BF16(0))

    def beside(own, value, parts):
        extra = jnp.where(
            spot == 0, parts[0], jnp.where(spot == 1, parts[1], jnp.where(spot == 2, parts[2], 0.0))
        )
        return jnp.where(own, value, extra.astype(BF16))

    grad_q = []
    grad_k = []
    grad_v = []
    heads = []
    for head in range(2):
        own = first if head == 0 else jnp.logical_not(first)
        delta = jnp.sum(jnp.where(own, product, 0.0), axis=1, keepdims=True)
        heads.append((own, beside(own, queries, logs), beside(own, grads, three_parts(delta))))
    total_q = [None, None]
    for at in range(0, rows, block):
        keys_in = k_ref[at : at + block, :]
        values = v_ref[at : at + block, :]
        out_k = []
        out_v = []
        for head, (own, queries_wide, grads_wide) in enumerate(heads):
            probs = jnp.exp(dot(jnp.where(own, keys_in, minus), queries_wide, NT))
            out_v.append(dot(probs.astype(BF16), grads))
            spread = dot(jnp.where(own, values, minus), grads_wide, NT)
            inner = (probs * spread).astype(BF16)
            out_k.append(dot(inner, queries))
            part = dot(inner, keys_in, TN)
            total_q[head] = part if total_q[head] is None else total_q[head] + part
        grad_k.append(jnp.where(first, out_k[0], out_k[1]).astype(BF16))
        grad_v.append(jnp.where(first, out_v[0], out_v[1]).astype(BF16))
    grad_q = (jnp.where(first, total_q[0], total_q[1]) * SCALE_FACTOR).astype(BF16)
    joined = jnp.concatenate(
        [grad_q, jnp.concatenate(grad_k, axis=0), jnp.concatenate(grad_v, axis=0)], axis=1
    )
    grad_out[...] = joined
    held[...] = dot(turned_ref[...], joined).astype(BF16)
    me = me_ref[0]
    for target, steps in zip(targets, leaving):
        for place, step in enumerate(steps):
            target[place * TILE : (place + 1) * TILE, :] = held[rows_at(me ^ step), :]
    sums_out[...] = jnp.sum(joined.astype(F32), axis=0, keepdims=True)


def attend_back(me, leaving, proj, grad_mixed, mixed, stats, turned, begin, count, before=(), block=256):
    rows, cols = proj.shape
    width = cols // 3
    pairs = width // PAIR
    column = pl.BlockSpec((rows, PAIR), lambda p: (0, begin + p))
    place = lambda p: (0, begin + p)
    tall = [len(steps) * TILE for steps in leaving]
    inputs = (me, proj, proj, proj, grad_mixed, mixed, stats, turned)
    return call(
        functools.partial(attend_back_kernel, block, leaving, len(before)),
        (count,),
        [
            pl.BlockSpec(memory_space=pltpu.SMEM),
            column,
            pl.BlockSpec((rows, PAIR), lambda p: (0, pairs + begin + p)),
            pl.BlockSpec((rows, PAIR), lambda p: (0, 2 * pairs + begin + p)),
            column,
            column,
            column,
            whole((width, rows)),
        ]
        + [pl.BlockSpec(memory_space=pl.ANY)] * len(before),
        [pl.BlockSpec((rows, 3 * PAIR), place), pl.BlockSpec((1, 3 * PAIR), place)]
        + [pl.BlockSpec((high, 3 * PAIR), place) for high in tall],
        [jax.ShapeDtypeStruct((rows, cols), BF16), jax.ShapeDtypeStruct((1, cols), F32)]
        + [jax.ShapeDtypeStruct((high, cols), BF16) for high in tall],
        count * (10 * rows * rows * PAIR + 6 * rows * width * PAIR),
        scratch=[pltpu.VMEM((width, 3 * PAIR), BF16)],
        exps=2 * count * rows * rows,
        name="attend_back",
        aliases={len(inputs) + k: k for k in range(len(before))},
    )(*inputs, *before)


ROOT_HALF = 0.7071067811865476
ROOT_TWO_PI = 0.3989422804014327


def feed_kernel(
    apart,
    leaving,
    me_ref,
    tok,
    mixed,
    cot,
    vec,
    b_up,
    *refs,
):
    sources = refs[: len(apart)]
    refs = refs[len(apart) :]
    output, grad_mid_out, grad_mixed_out = refs[:3]
    targets = refs[3 : 3 + len(leaving)]
    (
        sums_out,
        sums_up_out,
        w_out,
        w_up,
        w_down,
        acc_down,
        acc_up,
        acc_out,
        acc_sums,
        acc_sums_up,
    ) = refs[3 + len(leaving) :]
    step = pl.program_id(0)
    bias_out, gain, shift, bias_down = (
        vec[k : k + 1, :] for k in (BIAS_OUT, GAIN_F, SHIFT_F, BIAS_DOWN)
    )
    width = tok.shape[1]
    hidden = w_up.shape[1]
    folds = hidden // width
    edge = width + hidden
    me = me_ref[0]

    @pl.when(step == 0)
    def _():
        in_order(me, sources, apart, slice(0, width), w_out)
        in_order(me, sources, apart, slice(width, edge), w_up)
        for source, steps in zip(sources, apart):
            for block, far in enumerate(steps):
                for fold in range(folds):
                    w_down[rows_at((me ^ far) * folds + fold), :] = source[
                        block * TILE : (block + 1) * TILE,
                        edge + fold * width : edge + (fold + 1) * width,
                    ]

    start = tok[...].astype(F32) + vec[8:9, :]
    middle = start + dot(mixed[...], w_out[...]) + bias_out
    normed, inverse = normalize(middle)
    entry = (normed * gain + shift).astype(BF16)
    entry_t = entry.T
    cot_now = cot[...]
    cot_t = cot_now.T
    chunk = b_up.shape[1]
    result = middle + bias_down
    grad_feed = jnp.zeros_like(middle)

    @pl.when(step == 0)
    def _():
        acc_down[...] = jnp.zeros_like(acc_down)
        acc_up[...] = jnp.zeros_like(acc_up)
        acc_out[...] = jnp.zeros_like(acc_out)
        acc_sums[...] = jnp.zeros_like(acc_sums)
        acc_sums_up[...] = jnp.zeros_like(acc_sums_up)

    for at in range(0, hidden, chunk):
        up = w_up[:, at : at + chunk]
        down = w_down[at : at + chunk, :]
        row = at // chunk
        pre = dot(entry, up) + b_up[row : row + 1, :]
        cdf = 0.5 + 0.5 * lax.erf(pre * ROOT_HALF)
        act = (pre * cdf).astype(BF16)
        slope = cdf + pre * (ROOT_TWO_PI * jnp.exp(-0.5 * pre * pre))
        result = result + dot(act, down)
        acc_down[:, at : at + chunk] += dot(cot_t, act)
        grad_pre = (dot(cot_now, down, NT) * slope).astype(BF16)
        acc_up[:, at : at + chunk] += dot(entry_t, grad_pre)
        acc_sums_up[row : row + 1, :] += jnp.sum(grad_pre.astype(F32), axis=0, keepdims=True)
        grad_feed = grad_feed + dot(grad_pre, up, NT)
    output[...] = result.astype(BF16)
    grad_res = cot_now.astype(F32)
    grad_mid = grad_res + norm_back(grad_feed, gain, normed, inverse)
    grad_mid_out[...] = grad_mid
    branch = grad_mid.astype(BF16)
    grad_mixed_out[...] = dot(branch, w_out[...], NT).astype(BF16)
    acc_out[...] += dot(mixed[...].T, branch)
    for k, value in enumerate((grad_feed * normed, grad_feed, branch.astype(F32), grad_res)):
        acc_sums[k : k + 1, :] += jnp.sum(value, axis=0, keepdims=True)

    @pl.when(step == pl.num_programs(0) - 1)
    def _():
        for at in range(0, hidden, chunk):
            w_down[at : at + chunk, :] = acc_down[:, at : at + chunk].astype(BF16).T
        for target, steps in zip(targets, leaving):
            for block, far in enumerate(steps):
                spot = slice(block * TILE, (block + 1) * TILE)
                source = me ^ far
                target[spot, :width] = acc_out[rows_at(source), :].astype(BF16)
                target[spot, width:edge] = acc_up[rows_at(source), :].astype(BF16)
                for fold in range(folds):
                    target[spot, edge + fold * width : edge + (fold + 1) * width] = w_down[
                        rows_at(source * folds + fold), :
                    ]
        sums_out[...] = acc_sums[...]
        sums_up_out[...] = acc_sums_up[...]


def feed(me, tokens, mixed, cotangent, sources, apart, leaving, vec, b_up, block=256):
    rows, width = tokens.shape
    columns = sources[0].shape[1]
    hidden = (columns - width) // 2
    blocked = pl.BlockSpec((block, width), lambda i: (i, 0))
    return call(
        functools.partial(feed_kernel, apart, leaving),
        (rows // block,),
        [
            pl.BlockSpec(memory_space=pltpu.SMEM),
            blocked,
            blocked,
            blocked,
            whole(vec.shape),
            whole(b_up.shape),
        ]
        + [whole(source.shape) for source in sources],
        [
            blocked,
            blocked,
            blocked,
        ]
        + [whole((len(steps) * TILE, columns)) for steps in leaving]
        + [
            whole((8, width)),
            whole(b_up.shape),
        ],
        [
            jax.ShapeDtypeStruct((rows, width), BF16),
            jax.ShapeDtypeStruct((rows, width), F32),
            jax.ShapeDtypeStruct((rows, width), BF16),
        ]
        + [jax.ShapeDtypeStruct((len(steps) * TILE, columns), BF16) for steps in leaving]
        + [
            jax.ShapeDtypeStruct((8, width), F32),
            jax.ShapeDtypeStruct(b_up.shape, F32),
        ],
        12 * rows * width * hidden + 6 * rows * width * width,
        scratch=[
            pltpu.VMEM((width, width), BF16),
            pltpu.VMEM((width, hidden), BF16),
            pltpu.VMEM((hidden, width), BF16),
            pltpu.VMEM((width, hidden), F32),
            pltpu.VMEM((width, hidden), F32),
            pltpu.VMEM((width, width), F32),
            pltpu.VMEM((8, width), F32),
            pltpu.VMEM(b_up.shape, F32),
        ],
        exps=2 * rows * hidden,
        name="feed",
    )(me, tokens, mixed, cotangent, vec, b_up, *sources)


def finish_kernel(own, tok, vec, grad_mid, w, feed_sums, up_sums, proj_sums, grad_proj, grad_out, sums_out, acc):
    step = pl.program_id(0)
    normed, inverse = normalize(tok[...].astype(F32) + vec[8:9, :])
    width = tok.shape[1]
    pairs = width // PAIR
    folds = up_sums.shape[1] // LANES
    columns = [w[:, (kind * pairs + k) * PAIR : (kind * pairs + k + 1) * PAIR] for k in range(pairs) for kind in range(3)]
    grad_attn = dot(grad_proj[...], jnp.concatenate(columns, axis=1), NT)
    gain = vec[GAIN_A : GAIN_A + 1, :]
    grad_start = grad_mid[...] + norm_back(grad_attn, gain, normed, inverse)
    grad_out[...] = grad_start

    @pl.when(step == 0)
    def _():
        acc[...] = jnp.zeros_like(acc)

    for k, value in enumerate((grad_start, grad_attn * normed, grad_attn)):
        acc[k : k + 1, :] += jnp.sum(value, axis=0, keepdims=True)

    @pl.when(step == pl.num_programs(0) - 1)
    def _():
        acc[3:7, :] = feed_sums[0:4, :]
        up_high, up_low = split_two(up_sums[...])
        for fold in range(folds):
            place = folded_place(own, folds, fold, (LANES * folds, LANES), 1)
            rows = dot(up_high, place) + dot(up_low, place)
            for k in range(width // LANES):
                acc[7 + fold : 8 + fold, k * LANES : (k + 1) * LANES] = rows[k : k + 1, :]
        for k in range(pairs):
            acc[11:12, k * PAIR : (k + 1) * PAIR] = proj_sums[:, 3 * k * PAIR : (3 * k + 1) * PAIR]
            acc[12:13, k * PAIR : (k + 1) * PAIR] = proj_sums[
                :, (3 * k + 2) * PAIR : (3 * k + 3) * PAIR
            ]
        acc[TIME : TIME + 1, :] = vec[9:10, :]
        high, low = split_two(acc[...].T)
        half = acc.shape[0] // 2
        lane = lax.broadcasted_iota(jnp.int32, (1, acc.shape[0]), 1)
        shifted = pltpu.roll(low.astype(F32), half, 1)
        sums_out[...] = jnp.where(lane < half, high.astype(F32), shifted).astype(BF16)


TIME = 13


def finish(own, tokens, vec, grad_mid, w, feed_sums, up_sums, proj_sums, grad_proj, block=256):
    rows, width = tokens.shape
    blocked = pl.BlockSpec((block, width), lambda i: (i, 0))
    return call(
        functools.partial(finish_kernel, own),
        (rows // block,),
        [
            blocked,
            whole(vec.shape),
            blocked,
            whole(w.shape),
            whole(feed_sums.shape),
            whole(up_sums.shape),
            whole(proj_sums.shape),
            pl.BlockSpec((block, grad_proj.shape[1]), lambda i: (i, 0)),
        ],
        [blocked, whole((width, LANES))],
        [
            jax.ShapeDtypeStruct((rows, width), F32),
            jax.ShapeDtypeStruct((width, LANES), BF16),
        ],
        6 * rows * width * width,
        scratch=[pltpu.VMEM((LANES, width), F32)],
        name="finish",
    )(tokens, vec, grad_mid, w, feed_sums, up_sums, proj_sums, grad_proj)


SUM_ROWS = (1, 2, 3, 4, 11, 12, 5, 6)


def collect_kernel(folds, parts, *refs):
    vectors, up, table_out, held = refs[:-3], refs[-3], refs[-2], refs[-1]
    count, own, _ = parts.shape
    lane = lax.broadcasted_iota(jnp.int32, (1, LANES), 1).astype(F32)
    total = jnp.zeros((own, LANES), F32)
    table = jnp.zeros((own, LANES), F32)
    for source in range(count):
        part = parts[source].astype(F32)
        part = part + pltpu.roll(part, LANES // 2, 1)
        total = total + part
        table = table + jnp.where(lane == part[:, TIME : TIME + 1], part[:, 0:1], 0.0)
    held[...] = jnp.zeros_like(held)
    held[0:own, :] = total
    turned = held[...].T
    for k, out in zip(SUM_ROWS, vectors):
        out[...] = turned[k, 0:own]
    wide = turned[7:8, :]
    for fold in range(1, folds):
        wide = wide + pltpu.roll(turned[7 + fold : 8 + fold, :], fold * own, 1)
    up[...] = wide[0, 0 : folds * own]
    table_out[...] = table[:, 0 : table_out.shape[1]]


def collect(parts, steps, folds):
    own = parts.shape[1]
    vmem = pl.BlockSpec(memory_space=pltpu.VMEM)
    return pl.pallas_call(
        functools.partial(collect_kernel, folds),
        in_specs=[vmem],
        out_specs=[vmem] * 10,
        out_shape=[jax.ShapeDtypeStruct((own,), F32)] * 8
        + [jax.ShapeDtypeStruct((own * folds,), F32), jax.ShapeDtypeStruct((own, steps), F32)],
        scratch_shapes=[pltpu.VMEM((LANES, LANES), F32)],
        name="collect",
    )(parts)


def settle_kernel(count, *refs):
    parts, outs = refs[:count], refs[count:]
    value = parts[0][...].astype(F32)
    for part in parts[1:]:
        value = value + part[...].astype(F32)
    own = value.shape[0]
    if len(outs) == 1:
        pairs = value.shape[1] // (3 * PAIR)
        for pair in range(pairs):
            for kind in range(3):
                at = (3 * pair + kind) * PAIR
                spot = (kind * pairs + pair) * PAIR
                outs[0][:, spot : spot + PAIR] = value[:, at : at + PAIR]
    else:
        w_out, w_up, w_down = outs
        width = w_out.shape[1]
        edge = width + w_up.shape[1]
        w_out[...] = value[:, :width]
        w_up[...] = value[:, width:edge]
        for fold in range(w_down.shape[0] // own):
            w_down[fold * own : (fold + 1) * own, :] = value[:, edge + fold * width : edge + (fold + 1) * width]


def settle(parts, shapes, name):
    vmem = pl.BlockSpec(memory_space=pltpu.VMEM)
    return pl.pallas_call(
        functools.partial(settle_kernel, len(parts)),
        in_specs=[vmem] * len(parts),
        out_specs=[vmem] * len(shapes),
        out_shape=[jax.ShapeDtypeStruct(shape, F32) for shape in shapes],
        name=name,
    )(*parts)


def levels_of(count):
    bits = (count - 1).bit_length()
    if count != 1 << bits:
        raise ValueError("device count")
    return [[0]] + [list(range(at, min(at + 2, bits))) for at in range(1, bits, 2)]


def masks_of(bits):
    return [step << bits[0] for step in range(1 << len(bits))]


def permute(value, mask, count):
    return lax.ppermute(value, "dp", [(device, device ^ mask) for device in range(count)])


def gather_level(value, bits, count):
    return [value] + [permute(value, mask, count) for mask in masks_of(bits)[1:]]


def total(parts):
    result = parts[0].astype(F32)
    for part in parts[1:]:
        result = result + part.astype(F32)
    return result


def reduce_level(pieces, bits, count):
    return [pieces[0]] + [
        permute(piece, mask, count) for piece, mask in zip(pieces[1:], masks_of(bits)[1:])
    ]


def fold_down(rows, folds, own, back):
    width = rows.shape[1] // folds
    old, new = (TILE, own) if back else (own, TILE)
    rows = rows.reshape(-1, old, folds, width).transpose(0, 2, 1, 3)
    rows = rows.reshape(-1, folds, new, width).transpose(0, 2, 1, 3)
    return rows.reshape(-1, folds * width)


def refold(value, folded, folds, own, back):
    if not folded:
        return value
    edge = value.shape[1] - folded
    return jnp.concatenate([value[:, :edge], fold_down(value[:, edge:], folds, own, back)], axis=1)


class Plan:
    def __init__(self, count, own, folds):
        self.count, self.own, self.folds = count, own, folds
        self.levels = levels_of(count)
        self.tiled = own == TILE and len(self.levels) == 3
        index = lax.axis_index("dp").astype(jnp.int32)
        if self.tiled:
            near, middle, far = (masks_of(bits) for bits in self.levels)
            self.apart = tuple(
                tuple(a + b + c for c in far) for a in near for b in middle
            )
            self.leaving = tuple(tuple(a + b + c for b in middle for c in far) for a in near)
            self.me = index.reshape(1)
        else:
            self.index = index
            self.apart = self.leaving = (tuple(range(own * count // TILE)),)
            self.me = jnp.zeros((1,), jnp.int32)

    def spread(self, shard, level):
        return gather_level(shard, self.levels[level], self.count)

    def near(self, halves):
        keep, send = halves
        return keep, permute(send, 1, self.count)

    def cut(self, parts):
        size = parts[0].shape[0] // 4
        return [
            total([part[k * size : (k + 1) * size] for part in parts]).astype(BF16)
            for k in range(4)
        ]

    def around(self, pieces):
        return reduce_level(pieces, self.levels[1], self.count)

    def far(self, pieces):
        return reduce_level(pieces, self.levels[2], self.count)

    def whole(self, shard, folded):
        value = shard
        for bits in reversed(self.levels):
            value = jnp.stack(gather_level(value, bits, self.count))
        value = value.reshape((self.count,) + shard.shape)
        value = value[self.places() ^ self.place(self.index)]
        return refold(value.reshape(-1, shard.shape[1]), folded, self.folds, self.own, False)

    def place(self, device):
        result = 0
        for bits in self.levels:
            result = (result << len(bits)) | ((device >> bits[0]) & ((1 << len(bits)) - 1))
        return result

    def places(self):
        return self.place(jnp.arange(self.count, dtype=jnp.int32))

    def sum_whole(self, value, folded):
        value = refold(value, folded, self.folds, self.own, True)
        value = value.reshape(self.count, self.own, -1)
        order = [0] * self.count
        for device in range(self.count):
            order[self.place(device)] = device
        value = value[jnp.array(order, jnp.int32) ^ self.index]
        for at, bits in enumerate(self.levels):
            value = value.reshape((1 << len(bits), -1) + value.shape[1:])
            value = total(reduce_level(list(value), bits, self.count))
            if at < len(self.levels) - 1:
                value = value.astype(BF16)
        return value.reshape(self.own, -1)


def after(value, *done):
    leaves, tree = jax.tree.flatten(value)
    return jax.tree.unflatten(tree, lax.optimization_barrier((*leaves, *done))[: len(leaves)])


def exchange(value):
    return lax.all_to_all(value, "dp", 0, 0, tiled=True)


def per_device(
    count,
    tokens,
    timesteps,
    w_qkv,
    w_out,
    w_up,
    w_down,
    gain_attn,
    shift_attn,
    gain_ffn,
    shift_ffn,
    bias_query,
    bias_value,
    bias_out,
    bias_up,
    bias_down,
    step_table,
    cotangent,
):
    rows, width = tokens.shape
    own = width // count
    steps = step_table.shape[0]
    hidden = w_up.shape[1]
    folds = hidden // width
    edge = width + hidden
    plan = Plan(count, own, folds)
    pairs = width // PAIR

    vectors = (
        gain_attn,
        shift_attn,
        gain_ffn,
        shift_ffn,
        bias_query,
        bias_value,
        bias_out,
        bias_down,
    )
    entry = pack(w_qkv, step_table, vectors, bias_up)
    if plan.tiled:
        joint = join(w_out, w_up, w_down)
        far = plan.spread(entry, 2)
        joint = plan.spread(joint, 2)
        entry = jnp.concatenate(far, axis=0)
        entries = plan.spread(entry, 1)
        joint = jnp.concatenate(after(joint, *entries[1:]), axis=0)
        entries = entries + [permute(entry, 1, count) for entry in entries]
        joints = plan.spread(joint, 1)
    else:
        joint = jnp.concatenate(
            [w_out, w_up] + [w_down[k * own : (k + 1) * own] for k in range(folds)], axis=1
        )
        entries = [plan.whole(entry, 0)]
        joints = [plan.whole(joint, hidden)]

    proj, turned, full_qkv, vec, up_bias = project(
        plan.me, timesteps, tokens, entries, plan.apart, own, folds
    )
    mixed, stats = attend(proj)

    if plan.tiled:
        joints = after(joints, mixed)
        joints = joints + [permute(joint, 1, count) for joint in joints]
    feed_out = feed(
        plan.me, tokens, mixed, cotangent, joints, plan.apart, plan.leaving, vec, up_bias
    )
    output, grad_mid, grad_mixed = feed_out[:3]
    feed_sums, up_sums = feed_out[-2:]

    def back(grad_mixed, begin, number, before=()):
        return attend_back(
            plan.me, plan.leaving, proj, grad_mixed, mixed, stats, turned, begin, number, before
        )

    if plan.tiled:
        near = plan.near(feed_out[3:5])
        first = back(grad_mixed, 0, 1)
        pieces = plan.cut(after(near, first[0]))
        grad_proj, proj_sums, *leaving = back(after(grad_mixed, *pieces), 1, pairs - 1, first)
        pieces = plan.cut(after(plan.around(pieces), grad_proj))
        near = plan.near(leaving)
        grad_mid = after(grad_mid, *pieces)
        sum_parts = plan.far(pieces)
    else:
        grad_proj, proj_sums, leaving = back(grad_mixed, 0, pairs)
        sum_parts = [plan.sum_whole(feed_out[3], hidden)]
        weight_parts = [plan.sum_whole(leaving, 0)]

    grad_start, packed_sums = finish(
        own, tokens, vec, grad_mid, full_qkv, feed_sums, up_sums, proj_sums, grad_proj
    )
    parts = exchange(packed_sums.reshape(count, own, LANES))
    if plan.tiled:
        pieces = plan.around(plan.cut(after(near, grad_start)))
        weight_parts = plan.far(plan.cut(pieces))
    *sums, sum_up, sum_table = collect(parts, steps, folds)
    sum_out, sum_w_up, sum_down = settle(
        sum_parts, (w_out.shape, w_up.shape, w_down.shape), "settle_joint"
    )
    (sum_qkv,) = settle(weight_parts, (w_qkv.shape,), "settle_qkv")
    return (
        output,
        grad_start,
        sum_qkv,
        sum_out,
        sum_w_up,
        sum_down,
        *sums[:7],
        sum_up,
        sums[7],
        sum_table.T,
    )


def solution(mesh):
    in_specs = (
        P("dp", None),
        P("dp"),
        P("dp", None),
        P("dp", None),
        P("dp", None),
        P("dp", None),
        P("dp"),
        P("dp"),
        P("dp"),
        P("dp"),
        P("dp"),
        P("dp"),
        P("dp"),
        P("dp"),
        P("dp"),
        P(None, "dp"),
        P("dp", None),
    )
    out_specs = (
        P("dp", None),
        P("dp", None),
        P("dp", None),
        P("dp", None),
        P("dp", None),
        P("dp", None),
        P("dp"),
        P("dp"),
        P("dp"),
        P("dp"),
        P("dp"),
        P("dp"),
        P("dp"),
        P("dp"),
        P("dp"),
        P(None, "dp"),
    )
    return jax.shard_map(
        functools.partial(per_device, mesh.shape["dp"]), mesh=mesh, in_specs=in_specs, out_specs=out_specs, check_vma=False
    )
```

profile of v0, /device:TPU:0, one launch (start us, length us, event | category | flops | bytes accessed | tf_op | source)
XLA Modules:
  0.0 171.7 jit_solution(10089697839398097449)
XLA Ops:
  0.7 1.6 pack.1
  2.3 5.1 %collective-permute-start.2 = (bf16[16,1664]{1,0:T(8,128)(2,1)}, bf16[16,1664]{1,0:T(8,128)(2,1)S(1)}, u32[]{:S(2)}, u32[]{:S(2)}) collective-permute-start(bf16[16,1664]{1,0:T(8,128)(2,1)} %pack.1), channel_id=1, source_target_pairs={{0,24},{1,25},{2,26},{3,27},{4,28},{5,29},{6,30},{7,31},{8,16},{9,... | collective-permute-start | bytes 159752 | tf_op jit(solution)/shard_map/ppermute | solution.py:671
  7.9 1.6 join.1
  9.5 3.8 %collective-permute-start.12 = (bf16[16,4608]{1,0:T(8,128)(2,1)}, bf16[16,4608]{1,0:T(8,128)(2,1)S(1)}, u32[]{:S(2)}, u32[]{:S(2)}) collective-permute-start(bf16[16,4608]{1,0:T(8,128)(2,1)} %join.1), channel_id=1, source_target_pairs={{0,24},{1,25},{2,26},{3,27},{4,28},{5,29},{6,30},{7,31},{8,16},{9,... | collective-permute-start | bytes 442376 | tf_op jit(solution)/shard_map/ppermute | solution.py:671
  14.2 2.5 %collective-permute-start.5 = (bf16[64,1664]{1,0:T(8,128)(2,1)S(1)}, bf16[64,1664]{1,0:T(8,128)(2,1)S(1)}, u32[]{:S(2)}, u32[]{:S(2)}) collective-permute-start(bf16[64,1664]{1,0:T(8,128)(2,1)S(1)} %pad_maximum_fusion.refs_0_), channel_id=1, source_target_pairs={{0,6},{1,7},{2,4},{3,5},{4,2},{5,3},{6,0},{7,1},{8,14},{9,15},{10,... | collective-permute-start | bytes 638984 | tf_op jit(solution)/shard_map/ppermute | solution.py:671
  17.7 1.9 %collective-permute-start.11 = (bf16[16,4608]{1,0:T(8,128)(2,1)}, bf16[16,4608]{1,0:T(8,128)(2,1)S(1)}, u32[]{:S(2)}, u32[]{:S(2)}) collective-permute-start(bf16[16,4608]{1,0:T(8,128)(2,1)} %join.1), channel_id=1, source_target_pairs={{0,16},{1,17},{2,18},{3,19},{4,20},{5,21},{6,22},{7,23},{8,24},{9,... | collective-permute-start | bytes 442376 | tf_op jit(solution)/shard_map/ppermute | solution.py:671
  19.6 1.2 collective-permute-start.10
  20.8 4.6 %collective-permute-done.11 = bf16[16,4608]{1,0:T(8,128)(2,1)S(1)} collective-permute-done((bf16[16,4608]{1,0:T(8,128)(2,1)}, bf16[16,4608]{1,0:T(8,128)(2,1)S(1)}, u32[]{:S(2)}, u32[]{:S(2)}) %collective-permute-start.11) | collective-permute-done | bytes 147488 | tf_op jit(solution)/shard_map/ppermute | solution.py:671
  25.5 1.0 collective-permute-done.10
  26.5 1.1 constant_dynamic-update-slice_fusion.3
  27.8 2.5 %collective-permute-start.15 = (bf16[64,4608]{1,0:T(8,128)(2,1)S(1)}, bf16[64,4608]{1,0:T(8,128)(2,1)S(1)}, u32[]{:S(2)}, u32[]{:S(2)}) collective-permute-start(bf16[64,4608]{1,0:T(8,128)(2,1)S(1)} %constant_dynamic-update-slice_fusion.refs_0_), channel_id=1, source_target_pairs={{0,6},{1,7},{2,4},{3,5},{4,2},{5,3},{6,0},{7,1},{8,14},{9,15},{10,... | collective-permute-start | bytes 1769480 | tf_op jit(solution)/shard_map/ppermute | solution.py:671
  33.8 6.6 %project.1 = (bf16[1024,1536]{1,0:T(8,128)(2,1)}, bf16[512,1024]{1,0:T(8,128)(2,1)}, bf16[512,1536]{1,0:T(8,128)(2,1)}, f32[16,512]{1,0:T(8,128)}, f32[8,512]{1,0:T(8,128)}) custom-call(s32[1]{0:T(128)} %bitcast.me_ref, s32[1]{0:T(128)S(6)} %copy.44.time_ref, bf16[1024,512]{1,0:T(8,128)(2,1)} %tok.5, bf16[64,1664]{1,0:T(8,128)(2,1)} %copy-done.3, ...), custom_call_target="tpu_custom_call" | custom-call | flops 1610612736 | bytes 11632640 | tf_op jit(solution)/shard_map/project/pallas_call | solution.py:175
  40.4 13.8 %attend.1 = (bf16[1024,512]{1,0:T(8,128)(2,1)}, f32[1024,512]{1,0:T(8,128)}) custom-call(bf16[1024,1536]{1,0:T(8,128)(2,1)} %get-tuple-element.71.q_ref.k_ref.v_ref, bf16[1024,1536]{1,0:T(8,128)(2,1)} %get-tuple-element.71.q_ref.k_ref.v_ref, bf16[1024,1536]{1,0:T(8,128)(2,1)} %get-tuple-element.71.q_ref.k_ref.v_ref), custom_call_target="tpu_custom_call" | custom-call | flops 2147483648 | bytes 6291456 | tf_op jit(solution)/shard_map/attend/pallas_call | solution.py:228
  54.2 2.9 %collective-permute-done.14.refs_2_ = bf16[64,4608]{1,0:T(8,128)(2,1)S(1)} collective-permute-done((bf16[64,4608]{1,0:T(8,128)(2,1)S(1)}, bf16[64,4608]{1,0:T(8,128)(2,1)S(1)}, u32[]{:S(2)}, u32[]{:S(2)}) %collective-permute-start.14) | collective-permute-done | bytes 589856 | tf_op jit(solution)/shard_map/ppermute | solution.py:671
  62.6 30.1 %feed.1 = (bf16[1024,512]{1,0:T(8,128)(2,1)}, f32[1024,512]{1,0:T(8,128)}, bf16[1024,512]{1,0:T(8,128)(2,1)}, bf16[256,4608]{1,0:T(8,128)(2,1)}, bf16[256,4608]{...) custom-call(s32[1]{0:T(128)} %bitcast.me_ref, bf16[1024,512]{1,0:T(8,128)(2,1)} %tok.5, ...), custom_call_target="tpu_custom_call" | custom-call | flops 14495514624 | bytes 17891328 | tf_op jit(solution)/shard_map/feed/pallas_call | solution.py:466
  92.8 9.6 %attend_back.2 = (bf16[1024,1536]{1,0:T(8,128)(2,1)}, f32[1,1536]{1,0:T(1,128)}, bf16[256,1536]{1,0:T(8,128)(2,1)}, bf16[256,1536]{1,0:T(8,128)(2,1)}) custom-call(s32[1]{0:T(128)} %bitcast.me_ref, bf16[1024,1536]{1,0:T(8,128)(2,1)} %get-tuple-element.71.q_ref.k_ref.v_ref, bf16[1024,1536]{1,0:T(8,128)(2,1)} %get-tuple-element.71.q_ref.k_ref.v_ref, ...), custom_call_target="tpu_custom_call" | custom-call | flops 1744830464 | bytes 9449472 | tf_op jit(solution)/shard_map/attend_back/pallas_call | solution.py:321
  103.0 1.8 %collective-permute-start.23 = (bf16[64,4608]{1,0:T(8,128)(2,1)S(1)}, bf16[64,4608]{1,0:T(8,128)(2,1)S(1)}, u32[]{:S(2)}, u32[]{:S(2)}) collective-permute-start(bf16[64,4608]{1,0:T(8,128)(2,1)S(1)} %get-tuple-element.126), channel_id=1, source_target_pairs={{0,6},{1,7},{2,4},{3,5},{4,2},{5,3},{6,0},{7,1},{8,14},{9,15},{10,... | collective-permute-start | bytes 1769480 | tf_op jit(solution)/shard_map/ppermute | solution.py:671
  104.8 1.2 collective-permute-start.22
  106.6 23.8 %attend_back.3 = (bf16[1024,1536]{1,0:T(8,128)(2,1)}, f32[1,1536]{1,0:T(1,128)}, bf16[256,1536]{1,0:T(8,128)(2,1)}, bf16[256,1536]{1,0:T(8,128)(2,1)}) custom-call(s32[1]{0:T(128)} %bitcast.me_ref, bf16[1024,1536]{1,0:T(8,128)(2,1)} %get-tuple-element.71.q_ref.k_ref.v_ref, ...), custom_call_target="tpu_custom_call", output_to_operand_aliasing={{0}: (8, {}), {1}: (9, {}), {2}: (10, {}), {3}: (11, {})} | custom-call | flops 5234491392 | bytes 9449472 | tf_op jit(solution)/shard_map/attend_back/pallas_call | solution.py:321
  130.4 1.8 %collective-permute-done.22 = bf16[64,4608]{1,0:T(8,128)(2,1)S(1)} collective-permute-done((bf16[64,4608]{1,0:T(8,128)(2,1)S(1)}, bf16[64,4608]{1,0:T(8,128)(2,1)S(1)}, u32[]{:S(2)}, u32[]{:S(2)}) %collective-permute-start.22) | collective-permute-done | bytes 589856 | tf_op jit(solution)/shard_map/ppermute | solution.py:671
  133.2 7.6 %finish.1 = (f32[1024,512]{1,0:T(8,128)}, bf16[512,128]{1,0:T(8,128)(2,1)}) custom-call(bf16[1024,512]{1,0:T(8,128)(2,1)} %tok.5, f32[16,512]{1,0:T(8,128)} %get-tuple-element.73.vec, f32[1024,512]{1,0:T(8,128)} %get-tuple-element.102.grad_mid, bf16[512,1536]{1,0:T(8,128)(2,1)} %get-tuple-element.103.w, f32[8,512]{1,0:T(8,128)} %get-tuple-element.104.feed_sums, ...), custom_call_target="tpu_custom_call" | custom-call | flops 1610612736 | bytes 4456448 | tf_op jit(solution)/shard_map/finish/pallas_call | solution.py:561
  141.0 1.7 %collective-permute-start.27 = (bf16[64,1536]{1,0:T(8,128)(2,1)S(1)}, bf16[64,1536]{1,0:T(8,128)(2,1)S(1)}, u32[]{:S(2)}, u32[]{:S(2)}) collective-permute-start(bf16[64,1536]{1,0:T(8,128)(2,1)S(1)} %get-tuple-element.135), channel_id=1, source_target_pairs={{0,6},{1,7},{2,4},{3,5},{4,2},{5,3},{6,0},{7,1},{8,14},{9,15},{10,... | collective-permute-start | bytes 589832 | tf_op jit(solution)/shard_map/ppermute | solution.py:671
  142.8 1.2 collective-permute-start.26
  144.6 1.7 collective-permute-start.33
  146.3 4.4 %all-to-all-start = ((bf16[32,16,128]{2,1,0:T(8,128)(2,1)}), bf16[32,16,128]{2,1,0:T(8,128)(2,1)S(1)}, u32[]{:S(2)}, u32[]{:S(2)}) async-start(bf16[32,16,128]{2,1,0:T(8,128)(2,1)} %bitcast.2), calls=%async_computation | async-start | bytes 262144 | tf_op jit(solution)/shard_map/all_to_all | solution.py:782
  150.7 1.8 %collective-permute-start.31 = (bf16[16,4608]{1,0:T(8,128)(2,1)S(1)}, bf16[16,4608]{1,0:T(8,128)(2,1)S(1)}, u32[]{:S(2)}, u32[]{:S(2)}) collective-permute-start(bf16[16,4608]{1,0:T(8,128)(2,1)S(1)} %get-tuple-element.132), channel_id=1, source_target_pairs={{0,8},{1,9},{2,10},{3,11},{4,12},{5,13},{6,14},{7,15},{8,0},{9,1},... | collective-permute-start | bytes 442376 | tf_op jit(solution)/shard_map/ppermute | solution.py:671
  153.8 1.8 %collective-permute-start.30 = (bf16[16,1536]{1,0:T(8,128)(2,1)S(1)}, bf16[16,1536]{1,0:T(8,128)(2,1)S(1)}, u32[]{:S(2)}, u32[]{:S(2)}) collective-permute-start(bf16[16,1536]{1,0:T(8,128)(2,1)S(1)} %get-tuple-element.138), channel_id=1, source_target_pairs={{0,24},{1,25},{2,26},{3,27},{4,28},{5,29},{6,30},{7,31},{8,16},{9,... | collective-permute-start | bytes 147464 | tf_op jit(solution)/shard_map/ppermute | solution.py:671
  155.6 3.0 %collective-permute-start.28 = (bf16[16,1536]{1,0:T(8,128)(2,1)S(1)}, bf16[16,1536]{1,0:T(8,128)(2,1)S(1)}, u32[]{:S(2)}, u32[]{:S(2)}) collective-permute-start(bf16[16,1536]{1,0:T(8,128)(2,1)S(1)} %get-tuple-element.140), channel_id=1, source_target_pairs={{0,8},{1,9},{2,10},{3,11},{4,12},{5,13},{6,14},{7,15},{8,0},{9,1},... | collective-permute-start | bytes 147464 | tf_op jit(solution)/shard_map/ppermute | solution.py:671
  158.6 4.7 %collective-permute-done.32.refs_2_ = bf16[16,4608]{1,0:T(8,128)(2,1)S(1)} collective-permute-done((bf16[16,4608]{1,0:T(8,128)(2,1)S(1)}, bf16[16,4608]{1,0:T(8,128)(2,1)S(1)}, u32[]{:S(2)}, u32[]{:S(2)}) %collective-permute-start.32) | collective-permute-done | bytes 147488 | tf_op jit(solution)/shard_map/ppermute | solution.py:671
  164.7 1.9 %settle_joint.1 = (f32[16,512]{1,0:T(8,128)}, f32[16,2048]{1,0:T(8,128)}, f32[64,512]{1,0:T(8,128)}) custom-call(bf16[16,4608]{1,0:T(8,128)(2,1)} %get-tuple-element.133.refs_0_, bf16[16,4608]{1,0:T(8,128)(2,1)} %copy-done.6, bf16[16,4608]{1,0:T(8,128)(2,1)} %copy-done.5, bf16[16,4608]{1,0:T(8,128)(2,1)} %copy-done.4), custom_call_target="tpu_custom_call" | custom-call | tf_op jit(solution)/shard_map/settle_joint/pallas_call | solution.py:650
  167.2 2.3 %collect.1 = (f32[16]{0:T(128)}, f32[16]{0:T(128)}, f32[16]{0:T(128)}, f32[16]{0:T(128)}, f32[16]{0:T(128)}, /*index=5*/f32[16]{0:T(128)}, f32[16]{0:T(128)}, f32[16]{0:T(128)}, f32[64]{0:T(128)}, f32[16,50]{1,0:T(8,128)}) custom-call(bf16[32,16,128]{2,1,0:T(8,128)(2,1)} %copy-done.2), custom_call_target="tpu_custom_call" | custom-call | tf_op jit(solution)/shard_map/collect/pallas_call | solution.py:614
  170.2 1.5 settle_qkv.1
  (104 shorter events, 17.8 us)
Async XLA Ops:
  2.3 11.0 %collective-permute-start.2 = (bf16[16,1664]{1,0:T(8,128)(2,1)}, bf16[16,1664]{1,0:T(8,128)(2,1)S(1)}, u32[]{:S(2)}, u32[]{:S(2)}) collective-permute-start(bf16[16,1664]{1,0:T(8,128)(2,1)} %pack.1), channel_id=1, source_target_pairs={{0,24},{1,25},{2,26},{3,27},{4,28},{5,29},{6,30},{7,31},{8,16},{9,... | collective-permute-start | bytes 159752 | tf_op jit(solution)/shard_map/ppermute | solution.py:671
  7.4 6.0 %collective-permute-start.1 = (bf16[16,1664]{1,0:T(8,128)(2,1)}, bf16[16,1664]{1,0:T(8,128)(2,1)S(1)}, u32[]{:S(2)}, u32[]{:S(2)}) collective-permute-start(bf16[16,1664]{1,0:T(8,128)(2,1)} %pack.1), channel_id=1, source_target_pairs={{0,16},{1,17},{2,18},{3,19},{4,20},{5,21},{6,22},{7,23},{8,24},{9,... | collective-permute-start | bytes 159752 | tf_op jit(solution)/shard_map/ppermute | solution.py:671
  7.4 6.0 %collective-permute-start = (bf16[16,1664]{1,0:T(8,128)(2,1)}, bf16[16,1664]{1,0:T(8,128)(2,1)S(1)}, u32[]{:S(2)}, u32[]{:S(2)}) collective-permute-start(bf16[16,1664]{1,0:T(8,128)(2,1)} %pack.1), channel_id=1, source_target_pairs={{0,8},{1,9},{2,10},{3,11},{4,12},{5,13},{6,14},{7,15},{8,0},{9,1},... | collective-permute-start | bytes 159752 | tf_op jit(solution)/shard_map/ppermute | solution.py:671
  9.5 10.1 %collective-permute-start.12 = (bf16[16,4608]{1,0:T(8,128)(2,1)}, bf16[16,4608]{1,0:T(8,128)(2,1)S(1)}, u32[]{:S(2)}, u32[]{:S(2)}) collective-permute-start(bf16[16,4608]{1,0:T(8,128)(2,1)} %join.1), channel_id=1, source_target_pairs={{0,24},{1,25},{2,26},{3,27},{4,28},{5,29},{6,30},{7,31},{8,16},{9,... | collective-permute-start | bytes 442376 | tf_op jit(solution)/shard_map/ppermute | solution.py:671
  14.2 12.3 %collective-permute-start.5 = (bf16[64,1664]{1,0:T(8,128)(2,1)S(1)}, bf16[64,1664]{1,0:T(8,128)(2,1)S(1)}, u32[]{:S(2)}, u32[]{:S(2)}) collective-permute-start(bf16[64,1664]{1,0:T(8,128)(2,1)S(1)} %pad_maximum_fusion.refs_0_), channel_id=1, source_target_pairs={{0,6},{1,7},{2,4},{3,5},{4,2},{5,3},{6,0},{7,1},{8,14},{9,15},{10,... | collective-permute-start | bytes 638984 | tf_op jit(solution)/shard_map/ppermute | solution.py:671
  16.7 9.8 %collective-permute-start.4 = (bf16[64,1664]{1,0:T(8,128)(2,1)S(1)}, bf16[64,1664]{1,0:T(8,128)(2,1)S(1)}, u32[]{:S(2)}, u32[]{:S(2)}) collective-permute-start(bf16[64,1664]{1,0:T(8,128)(2,1)S(1)} %pad_maximum_fusion.refs_0_), channel_id=1, source_target_pairs={{0,4},{1,5},{2,6},{3,7},{4,0},{5,1},{6,2},{7,3},{8,12},{9,13},{10,... | collective-permute-start | bytes 638984 | tf_op jit(solution)/shard_map/ppermute | solution.py:671
  17.2 9.3 %collective-permute-start.3 = (bf16[64,1664]{1,0:T(8,128)(2,1)S(1)}, bf16[64,1664]{1,0:T(8,128)(2,1)S(1)}, u32[]{:S(2)}, u32[]{:S(2)}) collective-permute-start(bf16[64,1664]{1,0:T(8,128)(2,1)S(1)} %pad_maximum_fusion.refs_0_), channel_id=1, source_target_pairs={{0,2},{1,3},{2,0},{3,1},{4,6},{5,7},{6,4},{7,5},{8,10},{9,11},{10,... | collective-permute-start | bytes 638984 | tf_op jit(solution)/shard_map/ppermute | solution.py:671
  17.7 7.7 %collective-permute-start.11 = (bf16[16,4608]{1,0:T(8,128)(2,1)}, bf16[16,4608]{1,0:T(8,128)(2,1)S(1)}, u32[]{:S(2)}, u32[]{:S(2)}) collective-permute-start(bf16[16,4608]{1,0:T(8,128)(2,1)} %join.1), channel_id=1, source_target_pairs={{0,16},{1,17},{2,18},{3,19},{4,20},{5,21},{6,22},{7,23},{8,24},{9,... | collective-permute-start | bytes 442376 | tf_op jit(solution)/shard_map/ppermute | solution.py:671
  19.6 6.9 %collective-permute-start.10 = (bf16[16,4608]{1,0:T(8,128)(2,1)}, bf16[16,4608]{1,0:T(8,128)(2,1)S(1)}, u32[]{:S(2)}, u32[]{:S(2)}) collective-permute-start(bf16[16,4608]{1,0:T(8,128)(2,1)} %join.1), channel_id=1, source_target_pairs={{0,8},{1,9},{2,10},{3,11},{4,12},{5,13},{6,14},{7,15},{8,0},{9,1},... | collective-permute-start | bytes 442376 | tf_op jit(solution)/shard_map/ppermute | solution.py:671
  25.4 5.9 %collective-permute-start.6 = (bf16[64,1664]{1,0:T(8,128)(2,1)S(1)}, bf16[64,1664]{1,0:T(8,128)(2,1)S(1)}, u32[]{:S(2)}, u32[]{:S(2)}) collective-permute-start(bf16[64,1664]{1,0:T(8,128)(2,1)S(1)} %pad_maximum_fusion.refs_0_), channel_id=1, source_target_pairs={{0,1},{1,0},{2,3},{3,2},{4,5},{5,4},{6,7},{7,6},{8,9},{9,8},{10,11... | collective-permute-start | bytes 638984 | tf_op jit(solution)/shard_map/ppermute | solution.py:671
  27.7 3.7 %collective-permute-start.9 = (bf16[64,1664]{1,0:T(8,128)(2,1)S(1)}, bf16[64,1664]{1,0:T(8,128)(2,1)S(1)}, u32[]{:S(2)}, u32[]{:S(2)}) collective-permute-start(bf16[64,1664]{1,0:T(8,128)(2,1)S(1)} %collective-permute-done.5.refs_3_), channel_id=1, source_target_pairs={{0,1},{1,0},{2,3},{3,2},{4,5},{5,4},{6,7},{7,6},{8,9},{9,8},{10,11... | collective-permute-start | bytes 638984 | tf_op jit(solution)/shard_map/ppermute | solution.py:671
  27.8 26.4 %collective-permute-start.15 = (bf16[64,4608]{1,0:T(8,128)(2,1)S(1)}, bf16[64,4608]{1,0:T(8,128)(2,1)S(1)}, u32[]{:S(2)}, u32[]{:S(2)}) collective-permute-start(bf16[64,4608]{1,0:T(8,128)(2,1)S(1)} %constant_dynamic-update-slice_fusion.refs_0_), channel_id=1, source_target_pairs={{0,6},{1,7},{2,4},{3,5},{4,2},{5,3},{6,0},{7,1},{8,14},{9,15},{10,... | collective-permute-start | bytes 1769480 | tf_op jit(solution)/shard_map/ppermute | solution.py:671
  30.3 26.8 %collective-permute-start.14 = (bf16[64,4608]{1,0:T(8,128)(2,1)S(1)}, bf16[64,4608]{1,0:T(8,128)(2,1)S(1)}, u32[]{:S(2)}, u32[]{:S(2)}) collective-permute-start(bf16[64,4608]{1,0:T(8,128)(2,1)S(1)} %constant_dynamic-update-slice_fusion.refs_0_), channel_id=1, source_target_pairs={{0,4},{1,5},{2,6},{3,7},{4,0},{5,1},{6,2},{7,3},{8,12},{9,13},{10,... | collective-permute-start | bytes 1769480 | tf_op jit(solution)/shard_map/ppermute | solution.py:671
  30.8 26.4 %collective-permute-start.13 = (bf16[64,4608]{1,0:T(8,128)(2,1)S(1)}, bf16[64,4608]{1,0:T(8,128)(2,1)S(1)}, u32[]{:S(2)}, u32[]{:S(2)}) collective-permute-start(bf16[64,4608]{1,0:T(8,128)(2,1)S(1)} %constant_dynamic-update-slice_fusion.refs_0_), channel_id=1, source_target_pairs={{0,2},{1,3},{2,0},{3,1},{4,6},{5,7},{6,4},{7,5},{8,10},{9,11},{10,... | collective-permute-start | bytes 1769480 | tf_op jit(solution)/shard_map/ppermute | solution.py:671
  57.2 2.8 %collective-permute-start.17 = (bf16[64,4608]{1,0:T(8,128)(2,1)S(1)}, bf16[64,4608]{1,0:T(8,128)(2,1)S(1)}, u32[]{:S(2)}, u32[]{:S(2)}) collective-permute-start(bf16[64,4608]{1,0:T(8,128)(2,1)S(1)} %collective-permute-done.13.refs_1_), channel_id=1, source_target_pairs={{0,1},{1,0},{2,3},{3,2},{4,5},{5,4},{6,7},{7,6},{8,9},{9,8},{10,11... | collective-permute-start | bytes 1769480 | tf_op jit(solution)/shard_map/ppermute | solution.py:671
  57.7 3.2 %collective-permute-start.18 = (bf16[64,4608]{1,0:T(8,128)(2,1)S(1)}, bf16[64,4608]{1,0:T(8,128)(2,1)S(1)}, u32[]{:S(2)}, u32[]{:S(2)}) collective-permute-start(bf16[64,4608]{1,0:T(8,128)(2,1)S(1)} %collective-permute-done.14.refs_2_), channel_id=1, source_target_pairs={{0,1},{1,0},{2,3},{3,2},{4,5},{5,4},{6,7},{7,6},{8,9},{9,8},{10,11... | collective-permute-start | bytes 1769480 | tf_op jit(solution)/shard_map/ppermute | solution.py:671
  57.8 4.0 %collective-permute-start.19 = (bf16[64,4608]{1,0:T(8,128)(2,1)S(1)}, bf16[64,4608]{1,0:T(8,128)(2,1)S(1)}, u32[]{:S(2)}, u32[]{:S(2)}) collective-permute-start(bf16[64,4608]{1,0:T(8,128)(2,1)S(1)} %collective-permute-done.15.refs_3_), channel_id=1, source_target_pairs={{0,1},{1,0},{2,3},{3,2},{4,5},{5,4},{6,7},{7,6},{8,9},{9,8},{10,11... | collective-permute-start | bytes 1769480 | tf_op jit(solution)/shard_map/ppermute | solution.py:671
  92.6 9.8 %collective-permute-start.20 = (bf16[256,4608]{1,0:T(8,128)(2,1)}, bf16[256,4608]{1,0:T(8,128)(2,1)S(1)}, u32[]{:S(2)}, u32[]{:S(2)}) collective-permute-start(bf16[256,4608]{1,0:T(8,128)(2,1)} %get-tuple-element.86), channel_id=1, source_target_pairs={{0,1},{1,0},{2,3},{3,2},{4,5},{5,4},{6,7},{7,6},{8,9},{9,8},{10,11... | collective-permute-start | bytes 7077896 | tf_op jit(solution)/shard_map/ppermute | solution.py:671
  103.0 27.4 %collective-permute-start.23 = (bf16[64,4608]{1,0:T(8,128)(2,1)S(1)}, bf16[64,4608]{1,0:T(8,128)(2,1)S(1)}, u32[]{:S(2)}, u32[]{:S(2)}) collective-permute-start(bf16[64,4608]{1,0:T(8,128)(2,1)S(1)} %get-tuple-element.126), channel_id=1, source_target_pairs={{0,6},{1,7},{2,4},{3,5},{4,2},{5,3},{6,0},{7,1},{8,14},{9,15},{10,... | collective-permute-start | bytes 1769480 | tf_op jit(solution)/shard_map/ppermute | solution.py:671
  104.8 27.4 %collective-permute-start.22 = (bf16[64,4608]{1,0:T(8,128)(2,1)S(1)}, bf16[64,4608]{1,0:T(8,128)(2,1)S(1)}, u32[]{:S(2)}, u32[]{:S(2)}) collective-permute-start(bf16[64,4608]{1,0:T(8,128)(2,1)S(1)} %get-tuple-element.127), channel_id=1, source_target_pairs={{0,4},{1,5},{2,6},{3,7},{4,0},{5,1},{6,2},{7,3},{8,12},{9,13},{10,... | collective-permute-start | bytes 1769480 | tf_op jit(solution)/shard_map/ppermute | solution.py:671
  106.0 26.3 %collective-permute-start.21 = (bf16[64,4608]{1,0:T(8,128)(2,1)S(1)}, bf16[64,4608]{1,0:T(8,128)(2,1)S(1)}, u32[]{:S(2)}, u32[]{:S(2)}) collective-permute-start(bf16[64,4608]{1,0:T(8,128)(2,1)S(1)} %get-tuple-element.128), channel_id=1, source_target_pairs={{0,2},{1,3},{2,0},{3,1},{4,6},{5,7},{6,4},{7,5},{8,10},{9,11},{10,... | collective-permute-start | bytes 1769480 | tf_op jit(solution)/shard_map/ppermute | solution.py:671
  130.3 10.5 %collective-permute-start.24 = (bf16[256,1536]{1,0:T(8,128)(2,1)}, bf16[256,1536]{1,0:T(8,128)(2,1)S(1)}, u32[]{:S(2)}, u32[]{:S(2)}) collective-permute-start(bf16[256,1536]{1,0:T(8,128)(2,1)} %get-tuple-element.109), channel_id=1, source_target_pairs={{0,1},{1,0},{2,3},{3,2},{4,5},{5,4},{6,7},{7,6},{8,9},{9,8},{10,11... | collective-permute-start | bytes 2359304 | tf_op jit(solution)/shard_map/ppermute | solution.py:671
  141.0 9.6 %collective-permute-start.27 = (bf16[64,1536]{1,0:T(8,128)(2,1)S(1)}, bf16[64,1536]{1,0:T(8,128)(2,1)S(1)}, u32[]{:S(2)}, u32[]{:S(2)}) collective-permute-start(bf16[64,1536]{1,0:T(8,128)(2,1)S(1)} %get-tuple-element.135), channel_id=1, source_target_pairs={{0,6},{1,7},{2,4},{3,5},{4,2},{5,3},{6,0},{7,1},{8,14},{9,15},{10,... | collective-permute-start | bytes 589832 | tf_op jit(solution)/shard_map/ppermute | solution.py:671
  142.8 10.2 %collective-permute-start.26 = (bf16[64,1536]{1,0:T(8,128)(2,1)S(1)}, bf16[64,1536]{1,0:T(8,128)(2,1)S(1)}, u32[]{:S(2)}, u32[]{:S(2)}) collective-permute-start(bf16[64,1536]{1,0:T(8,128)(2,1)S(1)} %get-tuple-element.136), channel_id=1, source_target_pairs={{0,4},{1,5},{2,6},{3,7},{4,0},{5,1},{6,2},{7,3},{8,12},{9,13},{10,... | collective-permute-start | bytes 589832 | tf_op jit(solution)/shard_map/ppermute | solution.py:671
  144.0 9.1 %collective-permute-start.25 = (bf16[64,1536]{1,0:T(8,128)(2,1)S(1)}, bf16[64,1536]{1,0:T(8,128)(2,1)S(1)}, u32[]{:S(2)}, u32[]{:S(2)}) collective-permute-start(bf16[64,1536]{1,0:T(8,128)(2,1)S(1)} %get-tuple-element.137), channel_id=1, source_target_pairs={{0,2},{1,3},{2,0},{3,1},{4,6},{5,7},{6,4},{7,5},{8,10},{9,11},{10,... | collective-permute-start | bytes 589832 | tf_op jit(solution)/shard_map/ppermute | solution.py:671
  144.6 11.0 %collective-permute-start.33 = (bf16[16,4608]{1,0:T(8,128)(2,1)S(1)}, bf16[16,4608]{1,0:T(8,128)(2,1)S(1)}, u32[]{:S(2)}, u32[]{:S(2)}) collective-permute-start(bf16[16,4608]{1,0:T(8,128)(2,1)S(1)} %get-tuple-element.130), channel_id=1, source_target_pairs={{0,24},{1,25},{2,26},{3,27},{4,28},{5,29},{6,30},{7,31},{8,16},{9,... | collective-permute-start | bytes 442376 | tf_op jit(solution)/shard_map/ppermute | solution.py:671
  146.3 17.1 %collective-permute-start.32 = (bf16[16,4608]{1,0:T(8,128)(2,1)S(1)}, bf16[16,4608]{1,0:T(8,128)(2,1)S(1)}, u32[]{:S(2)}, u32[]{:S(2)}) collective-permute-start(bf16[16,4608]{1,0:T(8,128)(2,1)S(1)} %get-tuple-element.131), channel_id=1, source_target_pairs={{0,16},{1,17},{2,18},{3,19},{4,20},{5,21},{6,22},{7,23},{8,24},{9,... | collective-permute-start | bytes 442376 | tf_op jit(solution)/shard_map/ppermute | solution.py:671
  146.3 20.2 %all-to-all-start = ((bf16[32,16,128]{2,1,0:T(8,128)(2,1)}), bf16[32,16,128]{2,1,0:T(8,128)(2,1)S(1)}, u32[]{:S(2)}, u32[]{:S(2)}) async-start(bf16[32,16,128]{2,1,0:T(8,128)(2,1)} %bitcast.2), calls=%async_computation | async-start | bytes 262144 | tf_op jit(solution)/shard_map/all_to_all | solution.py:782
  150.7 12.7 %collective-permute-start.31 = (bf16[16,4608]{1,0:T(8,128)(2,1)S(1)}, bf16[16,4608]{1,0:T(8,128)(2,1)S(1)}, u32[]{:S(2)}, u32[]{:S(2)}) collective-permute-start(bf16[16,4608]{1,0:T(8,128)(2,1)S(1)} %get-tuple-element.132), channel_id=1, source_target_pairs={{0,8},{1,9},{2,10},{3,11},{4,12},{5,13},{6,14},{7,15},{8,0},{9,1},... | collective-permute-start | bytes 442376 | tf_op jit(solution)/shard_map/ppermute | solution.py:671
  153.8 15.8 %collective-permute-start.30 = (bf16[16,1536]{1,0:T(8,128)(2,1)S(1)}, bf16[16,1536]{1,0:T(8,128)(2,1)S(1)}, u32[]{:S(2)}, u32[]{:S(2)}) collective-permute-start(bf16[16,1536]{1,0:T(8,128)(2,1)S(1)} %get-tuple-element.138), channel_id=1, source_target_pairs={{0,24},{1,25},{2,26},{3,27},{4,28},{5,29},{6,30},{7,31},{8,16},{9,... | collective-permute-start | bytes 147464 | tf_op jit(solution)/shard_map/ppermute | solution.py:671
  155.6 13.9 %collective-permute-start.29 = (bf16[16,1536]{1,0:T(8,128)(2,1)S(1)}, bf16[16,1536]{1,0:T(8,128)(2,1)S(1)}, u32[]{:S(2)}, u32[]{:S(2)}) collective-permute-start(bf16[16,1536]{1,0:T(8,128)(2,1)S(1)} %get-tuple-element.139), channel_id=1, source_target_pairs={{0,16},{1,17},{2,18},{3,19},{4,20},{5,21},{6,22},{7,23},{8,24},{9,... | collective-permute-start | bytes 147464 | tf_op jit(solution)/shard_map/ppermute | solution.py:671
  155.6 13.9 %collective-permute-start.28 = (bf16[16,1536]{1,0:T(8,128)(2,1)S(1)}, bf16[16,1536]{1,0:T(8,128)(2,1)S(1)}, u32[]{:S(2)}, u32[]{:S(2)}) collective-permute-start(bf16[16,1536]{1,0:T(8,128)(2,1)S(1)} %get-tuple-element.140), channel_id=1, source_target_pairs={{0,8},{1,9},{2,10},{3,11},{4,12},{5,13},{6,14},{7,15},{8,0},{9,1},... | collective-permute-start | bytes 147464 | tf_op jit(solution)/shard_map/ppermute | solution.py:671
  (26 other events, 131.0 us)
where the time goes:
time: 172 us
  Pallas kernels  100 us (58%)
  starting transfers between devices  41.3 us (24%)
  waiting for transfers between devices  19.9 us (12%)
  local copies, waits for them, and re-layouts  5.27 us (3%)
  other arithmetic  3.21 us (2%)
    ppermute x34, starting transfers between devices, permute(): lax.ppermute(value, 'dp', [(device, device ^ mask) for device in range(co...  37 us
    pallas_call x2, Pallas kernels, attend_back(): call(functools.partial(attend_back_kernel, block, leaving, len(before)),...  33.4 us
    pallas_call x1, Pallas kernels, feed(): call(functools.partial(feed_kernel, apart, leaving), (rows // block,), [p...  30.1 us
    ppermute x34, waiting for transfers between devices, permute(): lax.ppermute(value, 'dp', [(device, device ^ mask) for device in range(co...  19.9 us
    pallas_call x1, Pallas kernels, attend(): call(functools.partial(attend_kernel, block), (pairs,), [pl.BlockSpec((ro...  13.8 us
    pallas_call x1, Pallas kernels, finish(): call(functools.partial(finish_kernel, own), (rows // block,), [blocked, w...  7.61 us
    pallas_call x1, Pallas kernels, project(): call(functools.partial(project_kernel, apart, own, folds), (rows // block...  6.63 us
    unnamed x49, local copies, waits for them, and re-layouts  5.26 us
  transfers between devices with their start and end apart: 35, of which 14 were waited for; matrix products, arithmetic and copies ran while one was open for 2% of the time, Pallas kernels for 39%

commit v1 on v0

--- a/solution.py
+++ b/solution.py
@@ -37,10 +37,14 @@
 
 def whole(shape):
     zeros = (0,) * len(shape)
-    return pl.BlockSpec(shape, lambda *_: zeros)
-
-
-def call(kernel, grid, in_specs, out_specs, out_shape, flops, scratch=(), exps=0, name=None, aliases=None):
+    return pl.BlockSpec(shape, lambda *_: zeros, pipeline_mode=pl.Buffered(1))
+
+
+def small(megabytes=4):
+    return pltpu.CompilerParams(vmem_limit_bytes=megabytes * 1024 * 1024)
+
+
+def call(kernel, grid, in_specs, out_specs, out_shape, flops, scratch=(), exps=0, name=None, aliases=None, vmem=56):
     moved = sum(s.size * s.dtype.itemsize for s in out_shape) * 2
     return pl.pallas_call(
         kernel,
@@ -50,7 +54,7 @@
         out_shape=out_shape,
         scratch_shapes=list(scratch),
         input_output_aliases=aliases or {},
-        compiler_params=pltpu.CompilerParams(vmem_limit_bytes=56 * 1024 * 1024),
+        compiler_params=pltpu.CompilerParams(vmem_limit_bytes=vmem * 1024 * 1024),
         cost_estimate=pl.CostEstimate(flops=flops, bytes_accessed=moved, transcendentals=exps),
         name=name,
     )
@@ -112,6 +116,25 @@
     )(w_out, w_up, w_down)
 
 
+def stack_kernel(*refs):
+    rows = refs[0].shape[0]
+    for k, part in enumerate(refs[:-1]):
+        refs[-1][k * rows : (k + 1) * rows, :] = part[...]
+
+
+def stack(parts):
+    rows, cols = parts[0].shape
+    vmem = pl.BlockSpec(memory_space=pltpu.VMEM)
+    return pl.pallas_call(
+        stack_kernel,
+        in_specs=[vmem] * len(parts),
+        out_specs=vmem,
+        out_shape=jax.ShapeDtypeStruct((rows * len(parts), cols), BF16),
+        compiler_params=small(),
+        name="stack",
+    )(*parts)
+
+
 def folded_place(own, folds, fold, shape, feature_axis):
     feature = lax.broadcasted_iota(jnp.int32, shape, feature_axis)
     unit = lax.broadcasted_iota(jnp.int32, shape, 1 - feature_axis)
@@ -137,15 +160,15 @@
 
 def project_kernel(apart, own, folds, me_ref, time_ref, tok, *refs):
     sources = refs[: len(apart)]
-    proj_out, turned_out, w_out, vec, b_up, small, held = refs[len(apart) :]
+    proj_out, turned_out, w_out, vec, b_up, tile, held = refs[len(apart) :]
     cols = w_out.shape[1]
 
     @pl.when(pl.program_id(0) == 0)
     def _():
         me = me_ref[0]
         in_order(me, sources, apart, slice(0, cols), w_out)
-        in_order(me, sources, apart, slice(cols, cols + LANES), small)
-        held[...] = small[...].astype(F32).T
+        in_order(me, sources, apart, slice(cols, cols + LANES), tile)
+        held[...] = tile[...].astype(F32).T
         vec[0:8, :] = held[64:72, :]
         vec[8:9, :] = held[pl.ds(time_ref[0], 1), :]
         vec[9:16, :] = jnp.full((7, vec.shape[1]), time_ref[0].astype(F32))
@@ -168,7 +191,7 @@
     proj_out[:, 2 * width :] = (product[:, 2 * width :] + vec[BIAS_V : BIAS_V + 1, :]).astype(BF16)
 
 
-def project(me, timesteps, tokens, sources, apart, own, folds, block=256):
+def project(me, timesteps, tokens, sources, apart, own, folds, block=512):
     rows, width = tokens.shape
     cols = sources[0].shape[1] - LANES
     smem = pl.BlockSpec(memory_space=pltpu.SMEM)
@@ -180,7 +203,7 @@
             smem,
             pl.BlockSpec((block, width), lambda i: (i, 0)),
         ]
-        + [whole(source.shape) for source in sources],
+        + [pl.BlockSpec(memory_space=pltpu.VMEM) for _ in sources],
         [
             pl.BlockSpec((block, cols), lambda i: (i, 0)),
             pl.BlockSpec((width, block), lambda i: (0, i)),
@@ -198,6 +221,7 @@
         2 * rows * width * cols,
         scratch=[pltpu.VMEM((width, LANES), BF16), pltpu.VMEM((LANES, width), F32)],
         name="project",
+        vmem=20,
     )(me, timesteps, tokens, *sources)
 
 
@@ -241,6 +265,7 @@
         4 * rows * rows * width,
         exps=rows * rows * width // HEAD_DIM,
         name="attend",
+        vmem=20,
     )(proj, proj, proj)
 
 
@@ -340,6 +365,7 @@
         scratch=[pltpu.VMEM((width, 3 * PAIR), BF16)],
         exps=2 * count * rows * rows,
         name="attend_back",
+        vmem=24,
         aliases={len(inputs) + k: k for k in range(len(before))},
     )(*inputs, *before)
 
@@ -369,11 +395,12 @@
         w_out,
         w_up,
         w_down,
-        acc_down,
         acc_up,
         acc_out,
         acc_sums,
         acc_sums_up,
+        result,
+        grad_acc,
     ) = refs[3 + len(leaving) :]
     step = pl.program_id(0)
     bias_out, gain, shift, bias_down = (
@@ -405,51 +432,46 @@
     cot_now = cot[...]
     cot_t = cot_now.T
     chunk = b_up.shape[1]
-    result = middle + bias_down
-    grad_feed = jnp.zeros_like(middle)
-
-    @pl.when(step == 0)
-    def _():
-        acc_down[...] = jnp.zeros_like(acc_down)
-        acc_up[...] = jnp.zeros_like(acc_up)
-        acc_out[...] = jnp.zeros_like(acc_out)
-        acc_sums[...] = jnp.zeros_like(acc_sums)
-        acc_sums_up[...] = jnp.zeros_like(acc_sums_up)
-
-    for at in range(0, hidden, chunk):
-        up = w_up[:, at : at + chunk]
-        down = w_down[at : at + chunk, :]
-        row = at // chunk
-        pre = dot(entry, up) + b_up[row : row + 1, :]
+    result[...] = middle + bias_down
+    grad_acc[...] = jnp.zeros_like(middle)
+    acc_sums[...] = jnp.zeros_like(acc_sums)
+    acc_sums_up[...] = jnp.zeros_like(acc_sums_up)
+
+    @pl.loop(0, hidden // chunk)
+    def _(row):
+        spot = pl.ds(pl.multiple_of(row * chunk, chunk), chunk)
+        up = w_up[:, spot]
+        down = w_down[spot, :]
+        pre = dot(entry, up) + b_up[pl.ds(row, 1), :]
         cdf = 0.5 + 0.5 * lax.erf(pre * ROOT_HALF)
         act = (pre * cdf).astype(BF16)
         slope = cdf + pre * (ROOT_TWO_PI * jnp.exp(-0.5 * pre * pre))
-        result = result + dot(act, down)
-        acc_down[:, at : at + chunk] += dot(cot_t, act)
+        result[...] += dot(act, down)
+        w_down[spot, :] = dot(cot_t, act).astype(BF16).T
         grad_pre = (dot(cot_now, down, NT) * slope).astype(BF16)
-        acc_up[:, at : at + chunk] += dot(entry_t, grad_pre)
-        acc_sums_up[row : row + 1, :] += jnp.sum(grad_pre.astype(F32), axis=0, keepdims=True)
-        grad_feed = grad_feed + dot(grad_pre, up, NT)
-    output[...] = result.astype(BF16)
+        acc_up[:, spot] = dot(entry_t, grad_pre).astype(BF16)
+        acc_sums_up[pl.ds(row, 1), :] = jnp.sum(grad_pre.astype(F32), axis=0, keepdims=True)
+        grad_acc[...] += dot(grad_pre, up, NT)
+
+    grad_feed = grad_acc[...]
+    output[...] = result[...].astype(BF16)
     grad_res = cot_now.astype(F32)
     grad_mid = grad_res + norm_back(grad_feed, gain, normed, inverse)
     grad_mid_out[...] = grad_mid
     branch = grad_mid.astype(BF16)
     grad_mixed_out[...] = dot(branch, w_out[...], NT).astype(BF16)
-    acc_out[...] += dot(mixed[...].T, branch)
+    acc_out[...] = dot(mixed[...].T, branch).astype(BF16)
     for k, value in enumerate((grad_feed * normed, grad_feed, branch.astype(F32), grad_res)):
-        acc_sums[k : k + 1, :] += jnp.sum(value, axis=0, keepdims=True)
+        acc_sums[k : k + 1, :] = jnp.sum(value, axis=0, keepdims=True)
 
     @pl.when(step == pl.num_programs(0) - 1)
     def _():
-        for at in range(0, hidden, chunk):
-            w_down[at : at + chunk, :] = acc_down[:, at : at + chunk].astype(BF16).T
         for target, steps in zip(targets, leaving):
             for block, far in enumerate(steps):
                 spot = slice(block * TILE, (block + 1) * TILE)
                 source = me ^ far
-                target[spot, :width] = acc_out[rows_at(source), :].astype(BF16)
-                target[spot, width:edge] = acc_up[rows_at(source), :].astype(BF16)
+                target[spot, :width] = acc_out[rows_at(source), :]
+                target[spot, width:edge] = acc_up[rows_at(source), :]
                 for fold in range(folds):
                     target[spot, edge + fold * width : edge + (fold + 1) * width] = w_down[
                         rows_at(source * folds + fold), :
@@ -458,8 +480,9 @@
         sums_up_out[...] = acc_sums_up[...]
 
 
-def feed(me, tokens, mixed, cotangent, sources, apart, leaving, vec, b_up, block=256):
+def feed(me, tokens, mixed, cotangent, sources, apart, leaving, vec, b_up):
     rows, width = tokens.shape
+    block = rows
     columns = sources[0].shape[1]
     hidden = (columns - width) // 2
     blocked = pl.BlockSpec((block, width), lambda i: (i, 0))
@@ -474,13 +497,13 @@
             whole(vec.shape),
             whole(b_up.shape),
         ]
-        + [whole(source.shape) for source in sources],
+        + [pl.BlockSpec(memory_space=pltpu.VMEM) for _ in sources],
         [
             blocked,
             blocked,
             blocked,
         ]
-        + [whole((len(steps) * TILE, columns)) for steps in leaving]
+        + [pl.BlockSpec(memory_space=pltpu.VMEM) for _ in leaving]
         + [
             whole((8, width)),
             whole(b_up.shape),
@@ -500,14 +523,16 @@
             pltpu.VMEM((width, width), BF16),
             pltpu.VMEM((width, hidden), BF16),
             pltpu.VMEM((hidden, width), BF16),
-            pltpu.VMEM((width, hidden), F32),
-            pltpu.VMEM((width, hidden), F32),
-            pltpu.VMEM((width, width), F32),
+            pltpu.VMEM((width, hidden), BF16),
+            pltpu.VMEM((width, width), BF16),
             pltpu.VMEM((8, width), F32),
             pltpu.VMEM(b_up.shape, F32),
+            pltpu.VMEM((rows, width), F32),
+            pltpu.VMEM((rows, width), F32),
         ],
         exps=2 * rows * hidden,
         name="feed",
+        vmem=46,
     )(me, tokens, mixed, cotangent, vec, b_up, *sources)
 
 
@@ -555,7 +580,7 @@
 TIME = 13
 
 
-def finish(own, tokens, vec, grad_mid, w, feed_sums, up_sums, proj_sums, grad_proj, block=256):
+def finish(own, tokens, vec, grad_mid, w, feed_sums, up_sums, proj_sums, grad_proj, block=512):
     rows, width = tokens.shape
     blocked = pl.BlockSpec((block, width), lambda i: (i, 0))
     return call(
@@ -579,6 +604,7 @@
         6 * rows * width * width,
         scratch=[pltpu.VMEM((LANES, width), F32)],
         name="finish",
+        vmem=20,
     )(tokens, vec, grad_mid, w, feed_sums, up_sums, proj_sums, grad_proj)
 
 
@@ -618,6 +644,7 @@
         out_shape=[jax.ShapeDtypeStruct((own,), F32)] * 8
         + [jax.ShapeDtypeStruct((own * folds,), F32), jax.ShapeDtypeStruct((own, steps), F32)],
         scratch_shapes=[pltpu.VMEM((LANES, LANES), F32)],
+        compiler_params=small(),
         name="collect",
     )(parts)
 
@@ -652,6 +679,7 @@
         in_specs=[vmem] * len(parts),
         out_specs=[vmem] * len(shapes),
         out_shape=[jax.ShapeDtypeStruct(shape, F32) for shape in shapes],
+        compiler_params=small(),
         name=name,
     )(*parts)
 
@@ -821,6 +849,8 @@
         bias_out,
         bias_down,
     )
+    plan.me = after(plan.me, w_qkv)
+    w_qkv = after(w_qkv, plan.me)
     entry = pack(w_qkv, step_table, vectors, bias_up)
     if plan.tiled:
         joint = join(w_out, w_up, w_down)
@@ -844,7 +874,7 @@
     mixed, stats = attend(proj)
 
     if plan.tiled:
-        joints = after(joints, mixed)
+        joints[1:] = after(joints[1:], mixed)
         joints = joints + [permute(joint, 1, count) for joint in joints]
     feed_out = feed(
         plan.me, tokens, mixed, cotangent, joints, plan.apart, plan.leaving, vec, up_bias
@@ -865,7 +895,6 @@
         pieces = plan.cut(after(plan.around(pieces), grad_proj))
         near = plan.near(leaving)
         grad_mid = after(grad_mid, *pieces)
-        sum_parts = plan.far(pieces)
     else:
         grad_proj, proj_sums, leaving = back(grad_mixed, 0, pairs)
         sum_parts = [plan.sum_whole(feed_out[3], hidden)]
@@ -876,6 +905,7 @@
     )
     parts = exchange(packed_sums.reshape(count, own, LANES))
     if plan.tiled:
+        sum_parts = plan.far(pieces)
         pieces = plan.around(plan.cut(after(near, grad_start)))
         weight_parts = plan.far(plan.cut(pieces))
     *sums, sum_up, sum_table = collect(parts, steps, folds)

time: 172 us -> 153 us (0.89)
  Pallas kernels: 100 us -> 78.8 us
  waiting for transfers between devices: 19.9 us -> 27.6 us
  local copies, waits for them, and re-layouts: 5.27 us -> 0.97 us
    pallas_call x1, Pallas kernels: 30.1 us -> 23 us  [feed(): call(functools.partial(feed_kernel, apart, leaving), (rows // block,), [p...]
    ppermute x34, waiting for transfers between devices: 19.9 us -> 26.2 us  [permute(): lax.ppermute(value, 'dp', [(device, device ^ mask) for device in range(co...]
    unnamed x49 -> x9, local copies, waits for them, and re-layouts: 5.26 us -> 0.96 us
    pallas_call x2, Pallas kernels: 33.4 us -> 29.1 us  [attend_back(): call(functools.partial(attend_back_kernel, block, leaving, len(before)),...]
    pallas_call x1, Pallas kernels: 6.63 us -> 3.12 us  [project(): call(functools.partial(project_kernel, apart, own, folds), (rows // block...]
    pallas_call x1, Pallas kernels: 7.61 us -> 4.68 us  [finish(): call(functools.partial(finish_kernel, own), (rows // block,), [blocked, w...]
    pallas_call x2, Pallas kernels: 3.4 us -> 1.41 us  [settle(): pl.pallas_call(functools.partial(settle_kernel, len(parts)), in_specs=[vm...]
  transfers between devices with their start and end apart: 35 -> 35, of which waited for: 14 -> 13; matrix products, arithmetic and copies ran while one was open for 2% -> 1% of each run, Pallas kernels for 39% -> 35%
where the time goes in v1:
time: 153 us
  Pallas kernels  78.8 us (52%)
  starting transfers between devices  41.7 us (27%)
  waiting for transfers between devices  27.6 us (18%)
  other arithmetic  2.01 us (1%)
  between operations  1.53 us (1%)
    ppermute x34, starting transfers between devices, permute(): lax.ppermute(value, 'dp', [(device, device ^ mask) for device in range(co...  37.3 us
    pallas_call x2, Pallas kernels, attend_back(): call(functools.partial(attend_back_kernel, block, leaving, len(before)),...  29.1 us
    ppermute x34, waiting for transfers between devices, permute(): lax.ppermute(value, 'dp', [(device, device ^ mask) for device in range(co...  26.2 us
    pallas_call x1, Pallas kernels, feed(): call(functools.partial(feed_kernel, apart, leaving), (rows // block,), [p...  23 us
    pallas_call x1, Pallas kernels, attend(): call(functools.partial(attend_kernel, block), (pairs,), [pl.BlockSpec((ro...  12.7 us
    pallas_call x1, Pallas kernels, finish(): call(functools.partial(finish_kernel, own), (rows // block,), [blocked, w...  4.68 us
    all_to_all x1, starting transfers between devices, exchange(): return lax.all_to_all(value, 'dp', 0, 0, tiled=True)  4.37 us
    pallas_call x1, Pallas kernels, project(): call(functools.partial(project_kernel, apart, own, folds), (rows // block...  3.12 us
  transfers between devices with their start and end apart: 35, of which 13 were waited for; matrix products, arithmetic and copies ran while one was open for 1% of the time, Pallas kernels for 35%

profile of v1, /device:TPU:0, one launch (start us, length us, event | category | flops | bytes accessed | tf_op | source)
XLA Modules:
  0.0 152.6 jit_solution(9411004758373258759)
XLA Ops:
  0.7 1.7 %pack.1 = bf16[16,1664]{1,0:T(8,128)(2,1)} custom-call(bf16[16,1536]{1,0:T(8,128)(2,1)} %w, bf16[16,50]{1,0:T(8,128)(2,1)} %bitcast.4, bf16[16]{0:T(256)(128)(2,1)} %refs_0_.1, bf16[16]{0:T(256)(128)(2,1)} %refs_1_.1, bf16[16]{0:T(256)(128)(2,1)} %refs_2_.1, bf16[16]{0:T(256)(128)(2,1)} %refs_3_.1, bf16[16]{0:T(256)(128)(2,1)} %refs_4_.1, ...), custom_call_target="tpu_custom_call" | custom-call | tf_op jit(solution)/shard_map/pack/pallas_call | solution.py:87
  2.4 5.1 %collective-permute-start.2 = (bf16[16,1664]{1,0:T(8,128)(2,1)}, bf16[16,1664]{1,0:T(8,128)(2,1)S(1)}, u32[]{:S(2)}, u32[]{:S(2)}) collective-permute-start(bf16[16,1664]{1,0:T(8,128)(2,1)} %pack.1), channel_id=1, source_target_pairs={{0,24},{1,25},{2,26},{3,27},{4,28},{5,29},{6,30},{7,31},{8,16},{9,... | collective-permute-start | bytes 159752 | tf_op jit(solution)/shard_map/ppermute | solution.py:699
  8.0 1.6 %join.1 = bf16[16,4608]{1,0:T(8,128)(2,1)} custom-call(bf16[16,512]{1,0:T(8,128)(2,1)} %w_out.1, bf16[16,2048]{1,0:T(8,128)(2,1)} %w_up.1, bf16[64,512]{1,0:T(8,128)(2,1)} %w_down.1), custom_call_target="tpu_custom_call" | custom-call | tf_op jit(solution)/shard_map/join/pallas_call | solution.py:110
  9.6 3.8 %collective-permute-start.12 = (bf16[16,4608]{1,0:T(8,128)(2,1)}, bf16[16,4608]{1,0:T(8,128)(2,1)S(1)}, u32[]{:S(2)}, u32[]{:S(2)}) collective-permute-start(bf16[16,4608]{1,0:T(8,128)(2,1)} %join.1), channel_id=1, source_target_pairs={{0,24},{1,25},{2,26},{3,27},{4,28},{5,29},{6,30},{7,31},{8,16},{9,... | collective-permute-start | bytes 442376 | tf_op jit(solution)/shard_map/ppermute | solution.py:699
  14.3 2.5 %collective-permute-start.5 = (bf16[64,1664]{1,0:T(8,128)(2,1)S(1)}, bf16[64,1664]{1,0:T(8,128)(2,1)S(1)}, u32[]{:S(2)}, u32[]{:S(2)}) collective-permute-start(bf16[64,1664]{1,0:T(8,128)(2,1)S(1)} %pad_maximum_fusion.refs_0_), channel_id=1, source_target_pairs={{0,6},{1,7},{2,4},{3,5},{4,2},{5,3},{6,0},{7,1},{8,14},{9,15},{10,... | collective-permute-start | bytes 638984 | tf_op jit(solution)/shard_map/ppermute | solution.py:699
  17.8 1.9 %collective-permute-start.11 = (bf16[16,4608]{1,0:T(8,128)(2,1)}, bf16[16,4608]{1,0:T(8,128)(2,1)S(1)}, u32[]{:S(2)}, u32[]{:S(2)}) collective-permute-start(bf16[16,4608]{1,0:T(8,128)(2,1)} %join.1), channel_id=1, source_target_pairs={{0,16},{1,17},{2,18},{3,19},{4,20},{5,21},{6,22},{7,23},{8,24},{9,... | collective-permute-start | bytes 442376 | tf_op jit(solution)/shard_map/ppermute | solution.py:699
  19.7 1.2 collective-permute-start.10
  20.9 4.6 %collective-permute-done.11 = bf16[16,4608]{1,0:T(8,128)(2,1)S(1)} collective-permute-done((bf16[16,4608]{1,0:T(8,128)(2,1)}, bf16[16,4608]{1,0:T(8,128)(2,1)S(1)}, u32[]{:S(2)}, u32[]{:S(2)}) %collective-permute-start.11) | collective-permute-done | bytes 147488 | tf_op jit(solution)/shard_map/ppermute | solution.py:699
  25.5 1.0 collective-permute-done.10
  26.6 0.9 constant_dynamic-update-slice_fusion.3
  27.7 2.5 %collective-permute-start.15 = (bf16[64,4608]{1,0:T(8,128)(2,1)S(1)}, bf16[64,4608]{1,0:T(8,128)(2,1)S(1)}, u32[]{:S(2)}, u32[]{:S(2)}) collective-permute-start(bf16[64,4608]{1,0:T(8,128)(2,1)S(1)} %constant_dynamic-update-slice_fusion.refs_0_), channel_id=1, source_target_pairs={{0,6},{1,7},{2,4},{3,5},{4,2},{5,3},{6,0},{7,1},{8,14},{9,15},{10,... | collective-permute-start | bytes 1769480 | tf_op jit(solution)/shard_map/ppermute | solution.py:699
  33.0 3.1 %project.1 = (bf16[1024,1536]{1,0:T(8,128)(2,1)S(1)}, bf16[512,1024]{1,0:T(8,128)(2,1)S(1)}, bf16[512,1536]{1,0:T(8,128)(2,1)S(1)}, f32[16,512]{1,0:T(8,128)S(1)}, f32[8,512]{1,0:T(8,128)S(1)}) custom-call(s32[1]{0:T(128)} %bitcast.me_ref, s32[1]{0:T(128)S(6)} %copy.44.time_ref, bf16[1024,512]{1,0:T(8,128)(2,1)S(1)} %copy-done.1, ...), custom_call_target="tpu_custom_call" | custom-call | flops 1610612736 | bytes 11632640 | tf_op jit(solution)/shard_map/project/pallas_call | solution.py:198
  36.1 12.7 %attend.1 = (bf16[1024,512]{1,0:T(8,128)(2,1)S(1)}, f32[1024,512]{1,0:T(8,128)S(1)}) custom-call(bf16[1024,1536]{1,0:T(8,128)(2,1)S(1)} %get-tuple-element.74.q_ref.k_ref.v_ref, bf16[1024,1536]{1,0:T(8,128)(2,1)S(1)} %get-tuple-element.74.q_ref.k_ref.v_ref, bf16[1024,1536]{1,0:T(8,128)(2,1)S(1)} %get-tuple-element.74.q_ref.k_ref.v_ref), custom_call_target="tpu_custom_call" | custom-call | flops 2147483648 | bytes 6291456 | tf_op jit(solution)/shard_map/attend/pallas_call | solution.py:252
  48.8 8.2 %collective-permute-done.14.refs_2_ = bf16[64,4608]{1,0:T(8,128)(2,1)S(1)} collective-permute-done((bf16[64,4608]{1,0:T(8,128)(2,1)S(1)}, bf16[64,4608]{1,0:T(8,128)(2,1)S(1)}, u32[]{:S(2)}, u32[]{:S(2)}) %collective-permute-start.14) | collective-permute-done | bytes 589856 | tf_op jit(solution)/shard_map/ppermute | solution.py:699
  57.6 1.5 collective-permute-done.17.refs_5_
  60.8 23.0 %feed.1 = (bf16[1024,512]{1,0:T(8,128)(2,1)}, f32[1024,512]{1,0:T(8,128)}, bf16[1024,512]{1,0:T(8,128)(2,1)S(1)}, bf16[256,4608]{1,0:T(8,128)(2,1)}, bf16[256,46...) custom-call(s32[1]{0:T(128)} %bitcast.me_ref, bf16[1024,512]{1,0:T(8,128)(2,1)S(1)} %copy-done.1, ...), custom_call_target="tpu_custom_call" | custom-call | flops 14495514624 | bytes 17891328 | tf_op jit(solution)/shard_map/feed/pallas_call | solution.py:489
  83.9 7.1 %attend_back.2 = (bf16[1024,1536]{1,0:T(8,128)(2,1)S(1)}, f32[1,1536]{1,0:T(1,128)S(1)}, bf16[256,1536]{1,0:T(8,128)(2,1)S(1)}, bf16[256,1536]{1,0:T(8,128)(2,1)S(1)}) custom-call(s32[1]{0:T(128)} %bitcast.me_ref, bf16[1024,1536]{1,0:T(8,128)(2,1)S(1)} %get-tuple-element.74.q_ref.k_ref.v_ref, bf16[1024,1536]{1,0:T(8,128)(2,1)S(1)} %get-tuple-element.74.q_ref.k_ref.v_ref, ...), custom_call_target="tpu_custom_call" | custom-call | flops 1744830464 | bytes 9449472 | tf_op jit(solution)/shard_map/attend_back/pallas_call | solution.py:346
  91.6 1.7 %collective-permute-start.23 = (bf16[64,4608]{1,0:T(8,128)(2,1)S(1)}, bf16[64,4608]{1,0:T(8,128)(2,1)S(1)}, u32[]{:S(2)}, u32[]{:S(2)}) collective-permute-start(bf16[64,4608]{1,0:T(8,128)(2,1)S(1)} %get-tuple-element.128), channel_id=1, source_target_pairs={{0,6},{1,7},{2,4},{3,5},{4,2},{5,3},{6,0},{7,1},{8,14},{9,15},{10,... | collective-permute-start | bytes 1769480 | tf_op jit(solution)/shard_map/ppermute | solution.py:699
  93.3 1.3 collective-permute-start.22
  95.1 22.0 %attend_back.3 = (bf16[1024,1536]{1,0:T(8,128)(2,1)S(1)}, f32[1,1536]{1,0:T(1,128)S(1)}, bf16[256,1536]{1,0:T(8,128)(2,1)S(1)}, bf16[256,1536]{1,0:T(8,128)(2,1)S(1)}) custom-call(s32[1]{0:T(128)} %bitcast.me_ref, ...), custom_call_target="tpu_custom_call", output_to_operand_aliasing={{0}: (8, {}), {1}: (9, {}), {2}: (10, {}), {3}: (11, {})} | custom-call | flops 5234491392 | bytes 9449472 | tf_op jit(solution)/shard_map/attend_back/pallas_call | solution.py:346
  117.3 3.5 %collective-permute-done.22 = bf16[64,4608]{1,0:T(8,128)(2,1)S(1)} collective-permute-done((bf16[64,4608]{1,0:T(8,128)(2,1)S(1)}, bf16[64,4608]{1,0:T(8,128)(2,1)S(1)}, u32[]{:S(2)}, u32[]{:S(2)}) %collective-permute-start.22) | collective-permute-done | bytes 589856 | tf_op jit(solution)/shard_map/ppermute | solution.py:699
  121.1 4.7 %finish.1 = (f32[1024,512]{1,0:T(8,128)}, bf16[512,128]{1,0:T(8,128)(2,1)}) custom-call(bf16[1024,512]{1,0:T(8,128)(2,1)S(1)} %copy-done.1, f32[16,512]{1,0:T(8,128)S(1)} %get-tuple-element.76.vec, f32[1024,512]{1,0:T(8,128)S(1)} %copy-done, bf16[512,1536]{1,0:T(8,128)(2,1)S(1)} %get-tuple-element.105.w, f32[8,512]{1,0:T(8,128)S(1)} %get-tuple-element.106.feed_sums, ...), custom_call_target="tpu_custom_call" | custom-call | flops 1610612736 | bytes 4456448 | tf_op jit(solution)/shard_map/finish/pallas_call | solution.py:586
  126.0 1.7 %collective-permute-start.27 = (bf16[64,1536]{1,0:T(8,128)(2,1)S(1)}, bf16[64,1536]{1,0:T(8,128)(2,1)S(1)}, u32[]{:S(2)}, u32[]{:S(2)}) collective-permute-start(bf16[64,1536]{1,0:T(8,128)(2,1)S(1)} %get-tuple-element.137), channel_id=1, source_target_pairs={{0,6},{1,7},{2,4},{3,5},{4,2},{5,3},{6,0},{7,1},{8,14},{9,15},{10,... | collective-permute-start | bytes 589832 | tf_op jit(solution)/shard_map/ppermute | solution.py:699
  127.7 1.3 collective-permute-start.26
  129.6 1.7 %collective-permute-start.33 = (bf16[16,4608]{1,0:T(8,128)(2,1)S(1)}, bf16[16,4608]{1,0:T(8,128)(2,1)S(1)}, u32[]{:S(2)}, u32[]{:S(2)}) collective-permute-start(bf16[16,4608]{1,0:T(8,128)(2,1)S(1)} %get-tuple-element.132), channel_id=1, source_target_pairs={{0,24},{1,25},{2,26},{3,27},{4,28},{5,29},{6,30},{7,31},{8,16},{9,... | collective-permute-start | bytes 442376 | tf_op jit(solution)/shard_map/ppermute | solution.py:699
  131.3 4.4 %all-to-all-start = ((bf16[32,16,128]{2,1,0:T(8,128)(2,1)}), bf16[32,16,128]{2,1,0:T(8,128)(2,1)S(1)}, u32[]{:S(2)}, u32[]{:S(2)}) async-start(bf16[32,16,128]{2,1,0:T(8,128)(2,1)} %bitcast.2), calls=%async_computation | async-start | bytes 262144 | tf_op jit(solution)/shard_map/all_to_all | solution.py:810
  135.7 1.8 %collective-permute-start.31 = (bf16[16,4608]{1,0:T(8,128)(2,1)S(1)}, bf16[16,4608]{1,0:T(8,128)(2,1)S(1)}, u32[]{:S(2)}, u32[]{:S(2)}) collective-permute-start(bf16[16,4608]{1,0:T(8,128)(2,1)S(1)} %get-tuple-element.134), channel_id=1, source_target_pairs={{0,8},{1,9},{2,10},{3,11},{4,12},{5,13},{6,14},{7,15},{8,0},{9,1},... | collective-permute-start | bytes 442376 | tf_op jit(solution)/shard_map/ppermute | solution.py:699
  138.2 1.9 %collective-permute-start.30 = (bf16[16,1536]{1,0:T(8,128)(2,1)S(1)}, bf16[16,1536]{1,0:T(8,128)(2,1)S(1)}, u32[]{:S(2)}, u32[]{:S(2)}) collective-permute-start(bf16[16,1536]{1,0:T(8,128)(2,1)S(1)} %get-tuple-element.140), channel_id=1, source_target_pairs={{0,24},{1,25},{2,26},{3,27},{4,28},{5,29},{6,30},{7,31},{8,16},{9,... | collective-permute-start | bytes 147464 | tf_op jit(solution)/shard_map/ppermute | solution.py:699
  140.2 3.4 %collective-permute-start.28 = (bf16[16,1536]{1,0:T(8,128)(2,1)S(1)}, bf16[16,1536]{1,0:T(8,128)(2,1)S(1)}, u32[]{:S(2)}, u32[]{:S(2)}) collective-permute-start(bf16[16,1536]{1,0:T(8,128)(2,1)S(1)} %get-tuple-element.142), channel_id=1, source_target_pairs={{0,8},{1,9},{2,10},{3,11},{4,12},{5,13},{6,14},{7,15},{8,0},{9,1},... | collective-permute-start | bytes 147464 | tf_op jit(solution)/shard_map/ppermute | solution.py:699
  143.6 4.7 %collective-permute-done.32.refs_2_ = bf16[16,4608]{1,0:T(8,128)(2,1)S(1)} collective-permute-done((bf16[16,4608]{1,0:T(8,128)(2,1)S(1)}, bf16[16,4608]{1,0:T(8,128)(2,1)S(1)}, u32[]{:S(2)}, u32[]{:S(2)}) %collective-permute-start.32) | collective-permute-done | bytes 147488 | tf_op jit(solution)/shard_map/ppermute | solution.py:699
  149.0 1.4 all-to-all-done.parts
  150.4 1.5 collect.1
  (64 shorter events, 11.5 us)
Async XLA Ops:
  2.4 11.0 %collective-permute-start.2 = (bf16[16,1664]{1,0:T(8,128)(2,1)}, bf16[16,1664]{1,0:T(8,128)(2,1)S(1)}, u32[]{:S(2)}, u32[]{:S(2)}) collective-permute-start(bf16[16,1664]{1,0:T(8,128)(2,1)} %pack.1), channel_id=1, source_target_pairs={{0,24},{1,25},{2,26},{3,27},{4,28},{5,29},{6,30},{7,31},{8,16},{9,... | collective-permute-start | bytes 159752 | tf_op jit(solution)/shard_map/ppermute | solution.py:699
  7.5 6.0 %collective-permute-start.1 = (bf16[16,1664]{1,0:T(8,128)(2,1)}, bf16[16,1664]{1,0:T(8,128)(2,1)S(1)}, u32[]{:S(2)}, u32[]{:S(2)}) collective-permute-start(bf16[16,1664]{1,0:T(8,128)(2,1)} %pack.1), channel_id=1, source_target_pairs={{0,16},{1,17},{2,18},{3,19},{4,20},{5,21},{6,22},{7,23},{8,24},{9,... | collective-permute-start | bytes 159752 | tf_op jit(solution)/shard_map/ppermute | solution.py:699
  7.5 6.0 %collective-permute-start = (bf16[16,1664]{1,0:T(8,128)(2,1)}, bf16[16,1664]{1,0:T(8,128)(2,1)S(1)}, u32[]{:S(2)}, u32[]{:S(2)}) collective-permute-start(bf16[16,1664]{1,0:T(8,128)(2,1)} %pack.1), channel_id=1, source_target_pairs={{0,8},{1,9},{2,10},{3,11},{4,12},{5,13},{6,14},{7,15},{8,0},{9,1},... | collective-permute-start | bytes 159752 | tf_op jit(solution)/shard_map/ppermute | solution.py:699
  9.6 10.1 %collective-permute-start.12 = (bf16[16,4608]{1,0:T(8,128)(2,1)}, bf16[16,4608]{1,0:T(8,128)(2,1)S(1)}, u32[]{:S(2)}, u32[]{:S(2)}) collective-permute-start(bf16[16,4608]{1,0:T(8,128)(2,1)} %join.1), channel_id=1, source_target_pairs={{0,24},{1,25},{2,26},{3,27},{4,28},{5,29},{6,30},{7,31},{8,16},{9,... | collective-permute-start | bytes 442376 | tf_op jit(solution)/shard_map/ppermute | solution.py:699
  14.3 12.3 %collective-permute-start.5 = (bf16[64,1664]{1,0:T(8,128)(2,1)S(1)}, bf16[64,1664]{1,0:T(8,128)(2,1)S(1)}, u32[]{:S(2)}, u32[]{:S(2)}) collective-permute-start(bf16[64,1664]{1,0:T(8,128)(2,1)S(1)} %pad_maximum_fusion.refs_0_), channel_id=1, source_target_pairs={{0,6},{1,7},{2,4},{3,5},{4,2},{5,3},{6,0},{7,1},{8,14},{9,15},{10,... | collective-permute-start | bytes 638984 | tf_op jit(solution)/shard_map/ppermute | solution.py:699
  16.8 9.8 %collective-permute-start.4 = (bf16[64,1664]{1,0:T(8,128)(2,1)S(1)}, bf16[64,1664]{1,0:T(8,128)(2,1)S(1)}, u32[]{:S(2)}, u32[]{:S(2)}) collective-permute-start(bf16[64,1664]{1,0:T(8,128)(2,1)S(1)} %pad_maximum_fusion.refs_0_), channel_id=1, source_target_pairs={{0,4},{1,5},{2,6},{3,7},{4,0},{5,1},{6,2},{7,3},{8,12},{9,13},{10,... | collective-permute-start | bytes 638984 | tf_op jit(solution)/shard_map/ppermute | solution.py:699
  17.3 9.3 %collective-permute-start.3 = (bf16[64,1664]{1,0:T(8,128)(2,1)S(1)}, bf16[64,1664]{1,0:T(8,128)(2,1)S(1)}, u32[]{:S(2)}, u32[]{:S(2)}) collective-permute-start(bf16[64,1664]{1,0:T(8,128)(2,1)S(1)} %pad_maximum_fusion.refs_0_), channel_id=1, source_target_pairs={{0,2},{1,3},{2,0},{3,1},{4,6},{5,7},{6,4},{7,5},{8,10},{9,11},{10,... | collective-permute-start | bytes 638984 | tf_op jit(solution)/shard_map/ppermute | solution.py:699
  17.8 7.7 %collective-permute-start.11 = (bf16[16,4608]{1,0:T(8,128)(2,1)}, bf16[16,4608]{1,0:T(8,128)(2,1)S(1)}, u32[]{:S(2)}, u32[]{:S(2)}) collective-permute-start(bf16[16,4608]{1,0:T(8,128)(2,1)} %join.1), channel_id=1, source_target_pairs={{0,16},{1,17},{2,18},{3,19},{4,20},{5,21},{6,22},{7,23},{8,24},{9,... | collective-permute-start | bytes 442376 | tf_op jit(solution)/shard_map/ppermute | solution.py:699
  19.7 6.9 %collective-permute-start.10 = (bf16[16,4608]{1,0:T(8,128)(2,1)}, bf16[16,4608]{1,0:T(8,128)(2,1)S(1)}, u32[]{:S(2)}, u32[]{:S(2)}) collective-permute-start(bf16[16,4608]{1,0:T(8,128)(2,1)} %join.1), channel_id=1, source_target_pairs={{0,8},{1,9},{2,10},{3,11},{4,12},{5,13},{6,14},{7,15},{8,0},{9,1},... | collective-permute-start | bytes 442376 | tf_op jit(solution)/shard_map/ppermute | solution.py:699
  25.5 5.7 %collective-permute-start.6 = (bf16[64,1664]{1,0:T(8,128)(2,1)S(1)}, bf16[64,1664]{1,0:T(8,128)(2,1)S(1)}, u32[]{:S(2)}, u32[]{:S(2)}) collective-permute-start(bf16[64,1664]{1,0:T(8,128)(2,1)S(1)} %pad_maximum_fusion.refs_0_), channel_id=1, source_target_pairs={{0,1},{1,0},{2,3},{3,2},{4,5},{5,4},{6,7},{7,6},{8,9},{9,8},{10,11... | collective-permute-start | bytes 638984 | tf_op jit(solution)/shard_map/ppermute | solution.py:699
  27.6 3.7 %collective-permute-start.9 = (bf16[64,1664]{1,0:T(8,128)(2,1)S(1)}, bf16[64,1664]{1,0:T(8,128)(2,1)S(1)}, u32[]{:S(2)}, u32[]{:S(2)}) collective-permute-start(bf16[64,1664]{1,0:T(8,128)(2,1)S(1)} %collective-permute-done.5.refs_3_), channel_id=1, source_target_pairs={{0,1},{1,0},{2,3},{3,2},{4,5},{5,4},{6,7},{7,6},{8,9},{9,8},{10,11... | collective-permute-start | bytes 638984 | tf_op jit(solution)/shard_map/ppermute | solution.py:699
  27.7 21.2 %collective-permute-start.15 = (bf16[64,4608]{1,0:T(8,128)(2,1)S(1)}, bf16[64,4608]{1,0:T(8,128)(2,1)S(1)}, u32[]{:S(2)}, u32[]{:S(2)}) collective-permute-start(bf16[64,4608]{1,0:T(8,128)(2,1)S(1)} %constant_dynamic-update-slice_fusion.refs_0_), channel_id=1, source_target_pairs={{0,6},{1,7},{2,4},{3,5},{4,2},{5,3},{6,0},{7,1},{8,14},{9,15},{10,... | collective-permute-start | bytes 1769480 | tf_op jit(solution)/shard_map/ppermute | solution.py:699
  30.2 26.8 %collective-permute-start.14 = (bf16[64,4608]{1,0:T(8,128)(2,1)S(1)}, bf16[64,4608]{1,0:T(8,128)(2,1)S(1)}, u32[]{:S(2)}, u32[]{:S(2)}) collective-permute-start(bf16[64,4608]{1,0:T(8,128)(2,1)S(1)} %constant_dynamic-update-slice_fusion.refs_0_), channel_id=1, source_target_pairs={{0,4},{1,5},{2,6},{3,7},{4,0},{5,1},{6,2},{7,3},{8,12},{9,13},{10,... | collective-permute-start | bytes 1769480 | tf_op jit(solution)/shard_map/ppermute | solution.py:699
  30.7 26.4 %collective-permute-start.13 = (bf16[64,4608]{1,0:T(8,128)(2,1)S(1)}, bf16[64,4608]{1,0:T(8,128)(2,1)S(1)}, u32[]{:S(2)}, u32[]{:S(2)}) collective-permute-start(bf16[64,4608]{1,0:T(8,128)(2,1)S(1)} %constant_dynamic-update-slice_fusion.refs_0_), channel_id=1, source_target_pairs={{0,2},{1,3},{2,0},{3,1},{4,6},{5,7},{6,4},{7,5},{8,10},{9,11},{10,... | collective-permute-start | bytes 1769480 | tf_op jit(solution)/shard_map/ppermute | solution.py:699
  32.7 24.9 %collective-permute-start.16 = (bf16[64,4608]{1,0:T(8,128)(2,1)S(1)}, bf16[64,4608]{1,0:T(8,128)(2,1)S(1)}, u32[]{:S(2)}, u32[]{:S(2)}) collective-permute-start(bf16[64,4608]{1,0:T(8,128)(2,1)S(1)} %constant_dynamic-update-slice_fusion.refs_0_), channel_id=1, source_target_pairs={{0,1},{1,0},{2,3},{3,2},{4,5},{5,4},{6,7},{7,6},{8,9},{9,8},{10,11... | collective-permute-start | bytes 1769480 | tf_op jit(solution)/shard_map/ppermute | solution.py:699
  57.1 2.8 %collective-permute-start.18 = (bf16[64,4608]{1,0:T(8,128)(2,1)S(1)}, bf16[64,4608]{1,0:T(8,128)(2,1)S(1)}, u32[]{:S(2)}, u32[]{:S(2)}) collective-permute-start(bf16[64,4608]{1,0:T(8,128)(2,1)S(1)} %collective-permute-done.14.refs_2_), channel_id=1, source_target_pairs={{0,1},{1,0},{2,3},{3,2},{4,5},{5,4},{6,7},{7,6},{8,9},{9,8},{10,11... | collective-permute-start | bytes 1769480 | tf_op jit(solution)/shard_map/ppermute | solution.py:699
  57.6 3.2 %collective-permute-start.19 = (bf16[64,4608]{1,0:T(8,128)(2,1)S(1)}, bf16[64,4608]{1,0:T(8,128)(2,1)S(1)}, u32[]{:S(2)}, u32[]{:S(2)}) collective-permute-start(bf16[64,4608]{1,0:T(8,128)(2,1)S(1)} %collective-permute-done.15.refs_3_), channel_id=1, source_target_pairs={{0,1},{1,0},{2,3},{3,2},{4,5},{5,4},{6,7},{7,6},{8,9},{9,8},{10,11... | collective-permute-start | bytes 1769480 | tf_op jit(solution)/shard_map/ppermute | solution.py:699
  83.8 7.2 %collective-permute-start.20 = (bf16[256,4608]{1,0:T(8,128)(2,1)}, bf16[256,4608]{1,0:T(8,128)(2,1)S(1)}, u32[]{:S(2)}, u32[]{:S(2)}) collective-permute-start(bf16[256,4608]{1,0:T(8,128)(2,1)} %get-tuple-element.88), channel_id=1, source_target_pairs={{0,1},{1,0},{2,3},{3,2},{4,5},{5,4},{6,7},{7,6},{8,9},{9,8},{10,11... | collective-permute-start | bytes 7077896 | tf_op jit(solution)/shard_map/ppermute | solution.py:699
  91.6 25.7 %collective-permute-start.23 = (bf16[64,4608]{1,0:T(8,128)(2,1)S(1)}, bf16[64,4608]{1,0:T(8,128)(2,1)S(1)}, u32[]{:S(2)}, u32[]{:S(2)}) collective-permute-start(bf16[64,4608]{1,0:T(8,128)(2,1)S(1)} %get-tuple-element.128), channel_id=1, source_target_pairs={{0,6},{1,7},{2,4},{3,5},{4,2},{5,3},{6,0},{7,1},{8,14},{9,15},{10,... | collective-permute-start | bytes 1769480 | tf_op jit(solution)/shard_map/ppermute | solution.py:699
  93.3 27.5 %collective-permute-start.22 = (bf16[64,4608]{1,0:T(8,128)(2,1)S(1)}, bf16[64,4608]{1,0:T(8,128)(2,1)S(1)}, u32[]{:S(2)}, u32[]{:S(2)}) collective-permute-start(bf16[64,4608]{1,0:T(8,128)(2,1)S(1)} %get-tuple-element.129), channel_id=1, source_target_pairs={{0,4},{1,5},{2,6},{3,7},{4,0},{5,1},{6,2},{7,3},{8,12},{9,13},{10,... | collective-permute-start | bytes 1769480 | tf_op jit(solution)/shard_map/ppermute | solution.py:699
  94.6 26.2 %collective-permute-start.21 = (bf16[64,4608]{1,0:T(8,128)(2,1)S(1)}, bf16[64,4608]{1,0:T(8,128)(2,1)S(1)}, u32[]{:S(2)}, u32[]{:S(2)}) collective-permute-start(bf16[64,4608]{1,0:T(8,128)(2,1)S(1)} %get-tuple-element.130), channel_id=1, source_target_pairs={{0,2},{1,3},{2,0},{3,1},{4,6},{5,7},{6,4},{7,5},{8,10},{9,11},{10,... | collective-permute-start | bytes 1769480 | tf_op jit(solution)/shard_map/ppermute | solution.py:699
  117.2 8.6 %collective-permute-start.24 = (bf16[256,1536]{1,0:T(8,128)(2,1)S(1)}, bf16[256,1536]{1,0:T(8,128)(2,1)S(1)}, u32[]{:S(2)}, u32[]{:S(2)}) collective-permute-start(bf16[256,1536]{1,0:T(8,128)(2,1)S(1)} %get-tuple-element.111), channel_id=1, source_target_pairs={{0,1},{1,0},{2,3},{3,2},{4,5},{5,4},{6,7},{7,6},{8,9},{9,8},{10,11... | collective-permute-start | bytes 2359304 | tf_op jit(solution)/shard_map/ppermute | solution.py:699
  126.0 9.7 %collective-permute-start.27 = (bf16[64,1536]{1,0:T(8,128)(2,1)S(1)}, bf16[64,1536]{1,0:T(8,128)(2,1)S(1)}, u32[]{:S(2)}, u32[]{:S(2)}) collective-permute-start(bf16[64,1536]{1,0:T(8,128)(2,1)S(1)} %get-tuple-element.137), channel_id=1, source_target_pairs={{0,6},{1,7},{2,4},{3,5},{4,2},{5,3},{6,0},{7,1},{8,14},{9,15},{10,... | collective-permute-start | bytes 589832 | tf_op jit(solution)/shard_map/ppermute | solution.py:699
  127.7 10.3 %collective-permute-start.26 = (bf16[64,1536]{1,0:T(8,128)(2,1)S(1)}, bf16[64,1536]{1,0:T(8,128)(2,1)S(1)}, u32[]{:S(2)}, u32[]{:S(2)}) collective-permute-start(bf16[64,1536]{1,0:T(8,128)(2,1)S(1)} %get-tuple-element.138), channel_id=1, source_target_pairs={{0,4},{1,5},{2,6},{3,7},{4,0},{5,1},{6,2},{7,3},{8,12},{9,13},{10,... | collective-permute-start | bytes 589832 | tf_op jit(solution)/shard_map/ppermute | solution.py:699
  129.1 9.0 %collective-permute-start.25 = (bf16[64,1536]{1,0:T(8,128)(2,1)S(1)}, bf16[64,1536]{1,0:T(8,128)(2,1)S(1)}, u32[]{:S(2)}, u32[]{:S(2)}) collective-permute-start(bf16[64,1536]{1,0:T(8,128)(2,1)S(1)} %get-tuple-element.139), channel_id=1, source_target_pairs={{0,2},{1,3},{2,0},{3,1},{4,6},{5,7},{6,4},{7,5},{8,10},{9,11},{10,... | collective-permute-start | bytes 589832 | tf_op jit(solution)/shard_map/ppermute | solution.py:699
  129.6 10.6 %collective-permute-start.33 = (bf16[16,4608]{1,0:T(8,128)(2,1)S(1)}, bf16[16,4608]{1,0:T(8,128)(2,1)S(1)}, u32[]{:S(2)}, u32[]{:S(2)}) collective-permute-start(bf16[16,4608]{1,0:T(8,128)(2,1)S(1)} %get-tuple-element.132), channel_id=1, source_target_pairs={{0,24},{1,25},{2,26},{3,27},{4,28},{5,29},{6,30},{7,31},{8,16},{9,... | collective-permute-start | bytes 442376 | tf_op jit(solution)/shard_map/ppermute | solution.py:699
  131.3 17.0 %collective-permute-start.32 = (bf16[16,4608]{1,0:T(8,128)(2,1)S(1)}, bf16[16,4608]{1,0:T(8,128)(2,1)S(1)}, u32[]{:S(2)}, u32[]{:S(2)}) collective-permute-start(bf16[16,4608]{1,0:T(8,128)(2,1)S(1)} %get-tuple-element.133), channel_id=1, source_target_pairs={{0,16},{1,17},{2,18},{3,19},{4,20},{5,21},{6,22},{7,23},{8,24},{9,... | collective-permute-start | bytes 442376 | tf_op jit(solution)/shard_map/ppermute | solution.py:699
  131.3 19.1 %all-to-all-start = ((bf16[32,16,128]{2,1,0:T(8,128)(2,1)}), bf16[32,16,128]{2,1,0:T(8,128)(2,1)S(1)}, u32[]{:S(2)}, u32[]{:S(2)}) async-start(bf16[32,16,128]{2,1,0:T(8,128)(2,1)} %bitcast.2), calls=%async_computation | async-start | bytes 262144 | tf_op jit(solution)/shard_map/all_to_all | solution.py:810
  135.7 12.6 %collective-permute-start.31 = (bf16[16,4608]{1,0:T(8,128)(2,1)S(1)}, bf16[16,4608]{1,0:T(8,128)(2,1)S(1)}, u32[]{:S(2)}, u32[]{:S(2)}) collective-permute-start(bf16[16,4608]{1,0:T(8,128)(2,1)S(1)} %get-tuple-element.134), channel_id=1, source_target_pairs={{0,8},{1,9},{2,10},{3,11},{4,12},{5,13},{6,14},{7,15},{8,0},{9,1},... | collective-permute-start | bytes 442376 | tf_op jit(solution)/shard_map/ppermute | solution.py:699
  138.2 13.7 %collective-permute-start.30 = (bf16[16,1536]{1,0:T(8,128)(2,1)S(1)}, bf16[16,1536]{1,0:T(8,128)(2,1)S(1)}, u32[]{:S(2)}, u32[]{:S(2)}) collective-permute-start(bf16[16,1536]{1,0:T(8,128)(2,1)S(1)} %get-tuple-element.140), channel_id=1, source_target_pairs={{0,24},{1,25},{2,26},{3,27},{4,28},{5,29},{6,30},{7,31},{8,16},{9,... | collective-permute-start | bytes 147464 | tf_op jit(solution)/shard_map/ppermute | solution.py:699
  140.1 11.8 %collective-permute-start.29 = (bf16[16,1536]{1,0:T(8,128)(2,1)S(1)}, bf16[16,1536]{1,0:T(8,128)(2,1)S(1)}, u32[]{:S(2)}, u32[]{:S(2)}) collective-permute-start(bf16[16,1536]{1,0:T(8,128)(2,1)S(1)} %get-tuple-element.141), channel_id=1, source_target_pairs={{0,16},{1,17},{2,18},{3,19},{4,20},{5,21},{6,22},{7,23},{8,24},{9,... | collective-permute-start | bytes 147464 | tf_op jit(solution)/shard_map/ppermute | solution.py:699
  140.2 11.7 %collective-permute-start.28 = (bf16[16,1536]{1,0:T(8,128)(2,1)S(1)}, bf16[16,1536]{1,0:T(8,128)(2,1)S(1)}, u32[]{:S(2)}, u32[]{:S(2)}) collective-permute-start(bf16[16,1536]{1,0:T(8,128)(2,1)S(1)} %get-tuple-element.142), channel_id=1, source_target_pairs={{0,8},{1,9},{2,10},{3,11},{4,12},{5,13},{6,14},{7,15},{8,0},{9,1},... | collective-permute-start | bytes 147464 | tf_op jit(solution)/shard_map/ppermute | solution.py:699
  (6 other events, 48.6 us)

commit v2 on v1

--- a/solution.py
+++ b/solution.py
@@ -893,8 +893,9 @@
         pieces = plan.cut(after(near, first[0]))
         grad_proj, proj_sums, *leaving = back(after(grad_mixed, *pieces), 1, pairs - 1, first)
         pieces = plan.cut(after(plan.around(pieces), grad_proj))
-        near = plan.near(leaving)
-        grad_mid = after(grad_mid, *pieces)
+        near = plan.near(after(leaving, *pieces))
+        leaving = plan.cut(near)
+        grad_mid = after(grad_mid, *leaving)
     else:
         grad_proj, proj_sums, leaving = back(grad_mixed, 0, pairs)
         sum_parts = [plan.sum_whole(feed_out[3], hidden)]
@@ -906,7 +907,7 @@
     parts = exchange(packed_sums.reshape(count, own, LANES))
     if plan.tiled:
         sum_parts = plan.far(pieces)
-        pieces = plan.around(plan.cut(after(near, grad_start)))
+        pieces = after(plan.around(leaving), grad_start)
         weight_parts = plan.far(plan.cut(pieces))
     *sums, sum_up, sum_table = collect(parts, steps, folds)
     sum_out, sum_w_up, sum_down = settle(

time: 153 us -> 153 us (level)
    ppermute x34, waiting for transfers between devices: 26.2 us -> 28.2 us  [permute(): lax.ppermute(value, 'dp', [(device, device ^ mask) for device in range(co...]
  transfers between devices with their start and end apart: 35 -> 35, of which waited for: 13 -> 14; matrix products, arithmetic and copies ran while one was open for 1% -> 1% of each run, Pallas kernels for 35% -> 35%
where the time goes in v2:
time: 153 us; the launch traced here: 152 us
  Pallas kernels  78.9 us (52%)
  starting transfers between devices  40.6 us (27%)
  waiting for transfers between devices  28.2 us (18%)
  other arithmetic  1.95 us (1%)
    ppermute x34, starting transfers between devices, permute(): lax.ppermute(value, 'dp', [(device, device ^ mask) for device in range(co...  36.2 us
    pallas_call x2, Pallas kernels, attend_back(): call(functools.partial(attend_back_kernel, block, leaving, len(before)),...  29.2 us
    ppermute x34, waiting for transfers between devices, permute(): lax.ppermute(value, 'dp', [(device, device ^ mask) for device in range(co...  28.2 us
    pallas_call x1, Pallas kernels, feed(): call(functools.partial(feed_kernel, apart, leaving), (rows // block,), [p...  23 us
    pallas_call x1, Pallas kernels, attend(): call(functools.partial(attend_kernel, block), (pairs,), [pl.BlockSpec((ro...  12.7 us
    pallas_call x1, Pallas kernels, finish(): call(functools.partial(finish_kernel, own), (rows // block,), [blocked, w...  4.69 us
    all_to_all x1, starting transfers between devices, exchange(): return lax.all_to_all(value, 'dp', 0, 0, tiled=True)  4.38 us
    pallas_call x1, Pallas kernels, project(): call(functools.partial(project_kernel, apart, own, folds), (rows // block...  3.12 us
  transfers between devices with their start and end apart: 35, of which 14 were waited for; matrix products, arithmetic and copies ran while one was open for 1% of the time, Pallas kernels for 35%

profile of v2, /device:TPU:0, one launch (start us, length us, event | category | flops | bytes accessed | tf_op | source)
XLA Modules:
  0.0 152.2 jit_solution(1573564619400847635)
XLA Ops:
  0.7 1.7 %pack.1 = bf16[16,1664]{1,0:T(8,128)(2,1)} custom-call(bf16[16,1536]{1,0:T(8,128)(2,1)} %w, bf16[16,50]{1,0:T(8,128)(2,1)} %bitcast.4, bf16[16]{0:T(256)(128)(2,1)} %refs_0_.1, bf16[16]{0:T(256)(128)(2,1)} %refs_1_.1, bf16[16]{0:T(256)(128)(2,1)} %refs_2_.1, bf16[16]{0:T(256)(128)(2,1)} %refs_3_.1, bf16[16]{0:T(256)(128)(2,1)} %refs_4_.1, ...), custom_call_target="tpu_custom_call" | custom-call | tf_op jit(solution)/shard_map/pack/pallas_call | solution.py:87
  2.4 5.1 %collective-permute-start.2 = (bf16[16,1664]{1,0:T(8,128)(2,1)}, bf16[16,1664]{1,0:T(8,128)(2,1)S(1)}, u32[]{:S(2)}, u32[]{:S(2)}) collective-permute-start(bf16[16,1664]{1,0:T(8,128)(2,1)} %pack.1), channel_id=1, source_target_pairs={{0,24},{1,25},{2,26},{3,27},{4,28},{5,29},{6,30},{7,31},{8,16},{9,... | collective-permute-start | bytes 159752 | tf_op jit(solution)/shard_map/ppermute | solution.py:699
  8.0 1.6 %join.1 = bf16[16,4608]{1,0:T(8,128)(2,1)} custom-call(bf16[16,512]{1,0:T(8,128)(2,1)} %w_out.1, bf16[16,2048]{1,0:T(8,128)(2,1)} %w_up.1, bf16[64,512]{1,0:T(8,128)(2,1)} %w_down.1), custom_call_target="tpu_custom_call" | custom-call | tf_op jit(solution)/shard_map/join/pallas_call | solution.py:110
  9.6 3.8 %collective-permute-start.12 = (bf16[16,4608]{1,0:T(8,128)(2,1)}, bf16[16,4608]{1,0:T(8,128)(2,1)S(1)}, u32[]{:S(2)}, u32[]{:S(2)}) collective-permute-start(bf16[16,4608]{1,0:T(8,128)(2,1)} %join.1), channel_id=1, source_target_pairs={{0,24},{1,25},{2,26},{3,27},{4,28},{5,29},{6,30},{7,31},{8,16},{9,... | collective-permute-start | bytes 442376 | tf_op jit(solution)/shard_map/ppermute | solution.py:699
  14.3 2.5 %collective-permute-start.5 = (bf16[64,1664]{1,0:T(8,128)(2,1)S(1)}, bf16[64,1664]{1,0:T(8,128)(2,1)S(1)}, u32[]{:S(2)}, u32[]{:S(2)}) collective-permute-start(bf16[64,1664]{1,0:T(8,128)(2,1)S(1)} %pad_maximum_fusion.refs_0_), channel_id=1, source_target_pairs={{0,6},{1,7},{2,4},{3,5},{4,2},{5,3},{6,0},{7,1},{8,14},{9,15},{10,... | collective-permute-start | bytes 638984 | tf_op jit(solution)/shard_map/ppermute | solution.py:699
  17.8 1.9 %collective-permute-start.11 = (bf16[16,4608]{1,0:T(8,128)(2,1)}, bf16[16,4608]{1,0:T(8,128)(2,1)S(1)}, u32[]{:S(2)}, u32[]{:S(2)}) collective-permute-start(bf16[16,4608]{1,0:T(8,128)(2,1)} %join.1), channel_id=1, source_target_pairs={{0,16},{1,17},{2,18},{3,19},{4,20},{5,21},{6,22},{7,23},{8,24},{9,... | collective-permute-start | bytes 442376 | tf_op jit(solution)/shard_map/ppermute | solution.py:699
  19.7 1.2 collective-permute-start.10
  20.9 4.6 %collective-permute-done.11 = bf16[16,4608]{1,0:T(8,128)(2,1)S(1)} collective-permute-done((bf16[16,4608]{1,0:T(8,128)(2,1)}, bf16[16,4608]{1,0:T(8,128)(2,1)S(1)}, u32[]{:S(2)}, u32[]{:S(2)}) %collective-permute-start.11) | collective-permute-done | bytes 147488 | tf_op jit(solution)/shard_map/ppermute | solution.py:699
  25.5 1.0 collective-permute-done.10
  26.6 0.9 constant_dynamic-update-slice_fusion.3
  27.7 2.5 %collective-permute-start.15 = (bf16[64,4608]{1,0:T(8,128)(2,1)S(1)}, bf16[64,4608]{1,0:T(8,128)(2,1)S(1)}, u32[]{:S(2)}, u32[]{:S(2)}) collective-permute-start(bf16[64,4608]{1,0:T(8,128)(2,1)S(1)} %constant_dynamic-update-slice_fusion.refs_0_), channel_id=1, source_target_pairs={{0,6},{1,7},{2,4},{3,5},{4,2},{5,3},{6,0},{7,1},{8,14},{9,15},{10,... | collective-permute-start | bytes 1769480 | tf_op jit(solution)/shard_map/ppermute | solution.py:699
  33.0 3.1 %project.1 = (bf16[1024,1536]{1,0:T(8,128)(2,1)S(1)}, bf16[512,1024]{1,0:T(8,128)(2,1)S(1)}, bf16[512,1536]{1,0:T(8,128)(2,1)S(1)}, f32[16,512]{1,0:T(8,128)S(1)}, f32[8,512]{1,0:T(8,128)S(1)}) custom-call(s32[1]{0:T(128)} %bitcast.me_ref, s32[1]{0:T(128)S(6)} %copy.44.time_ref, bf16[1024,512]{1,0:T(8,128)(2,1)S(1)} %copy-done.1, ...), custom_call_target="tpu_custom_call" | custom-call | flops 1610612736 | bytes 11632640 | tf_op jit(solution)/shard_map/project/pallas_call | solution.py:198
  36.1 12.7 %attend.1 = (bf16[1024,512]{1,0:T(8,128)(2,1)S(1)}, f32[1024,512]{1,0:T(8,128)S(1)}) custom-call(bf16[1024,1536]{1,0:T(8,128)(2,1)S(1)} %get-tuple-element.78.q_ref.k_ref.v_ref, bf16[1024,1536]{1,0:T(8,128)(2,1)S(1)} %get-tuple-element.78.q_ref.k_ref.v_ref, bf16[1024,1536]{1,0:T(8,128)(2,1)S(1)} %get-tuple-element.78.q_ref.k_ref.v_ref), custom_call_target="tpu_custom_call" | custom-call | flops 2147483648 | bytes 6291456 | tf_op jit(solution)/shard_map/attend/pallas_call | solution.py:252
  48.8 8.1 %collective-permute-done.14.refs_2_ = bf16[64,4608]{1,0:T(8,128)(2,1)S(1)} collective-permute-done((bf16[64,4608]{1,0:T(8,128)(2,1)S(1)}, bf16[64,4608]{1,0:T(8,128)(2,1)S(1)}, u32[]{:S(2)}, u32[]{:S(2)}) %collective-permute-start.14) | collective-permute-done | bytes 589856 | tf_op jit(solution)/shard_map/ppermute | solution.py:699
  57.6 1.5 collective-permute-done.17.refs_5_
  60.8 23.0 %feed.1 = (bf16[1024,512]{1,0:T(8,128)(2,1)}, f32[1024,512]{1,0:T(8,128)}, bf16[1024,512]{1,0:T(8,128)(2,1)S(1)}, bf16[256,4608]{1,0:T(8,128)(2,1)}, bf16[256,46...) custom-call(s32[1]{0:T(128)} %bitcast.me_ref, bf16[1024,512]{1,0:T(8,128)(2,1)S(1)} %copy-done.1, ...), custom_call_target="tpu_custom_call" | custom-call | flops 14495514624 | bytes 17891328 | tf_op jit(solution)/shard_map/feed/pallas_call | solution.py:489
  83.9 7.1 %attend_back.2 = (bf16[1024,1536]{1,0:T(8,128)(2,1)S(1)}, f32[1,1536]{1,0:T(1,128)S(1)}, bf16[256,1536]{1,0:T(8,128)(2,1)S(1)}, bf16[256,1536]{1,0:T(8,128)(2,1)S(1)}) custom-call(s32[1]{0:T(128)} %bitcast.me_ref, bf16[1024,1536]{1,0:T(8,128)(2,1)S(1)} %get-tuple-element.78.q_ref.k_ref.v_ref, bf16[1024,1536]{1,0:T(8,128)(2,1)S(1)} %get-tuple-element.78.q_ref.k_ref.v_ref, ...), custom_call_target="tpu_custom_call" | custom-call | flops 1744830464 | bytes 9449472 | tf_op jit(solution)/shard_map/attend_back/pallas_call | solution.py:346
  91.6 1.7 %collective-permute-start.23 = (bf16[64,4608]{1,0:T(8,128)(2,1)S(1)}, bf16[64,4608]{1,0:T(8,128)(2,1)S(1)}, u32[]{:S(2)}, u32[]{:S(2)}) collective-permute-start(bf16[64,4608]{1,0:T(8,128)(2,1)S(1)} %get-tuple-element.136), channel_id=1, source_target_pairs={{0,6},{1,7},{2,4},{3,5},{4,2},{5,3},{6,0},{7,1},{8,14},{9,15},{10,... | collective-permute-start | bytes 1769480 | tf_op jit(solution)/shard_map/ppermute | solution.py:699
  93.3 1.3 collective-permute-start.22
  95.2 22.1 %attend_back.3 = (bf16[1024,1536]{1,0:T(8,128)(2,1)S(1)}, f32[1,1536]{1,0:T(1,128)S(1)}, bf16[256,1536]{1,0:T(8,128)(2,1)S(1)}, bf16[256,1536]{1,0:T(8,128)(2,1)S(1)}) custom-call(s32[1]{0:T(128)} %bitcast.me_ref, ...), custom_call_target="tpu_custom_call", output_to_operand_aliasing={{0}: (8, {}), {1}: (9, {}), {2}: (10, {}), {3}: (11, {})} | custom-call | flops 5234491392 | bytes 9449472 | tf_op jit(solution)/shard_map/attend_back/pallas_call | solution.py:346
  117.3 3.6 %collective-permute-done.22 = bf16[64,4608]{1,0:T(8,128)(2,1)S(1)} collective-permute-done((bf16[64,4608]{1,0:T(8,128)(2,1)S(1)}, bf16[64,4608]{1,0:T(8,128)(2,1)S(1)}, u32[]{:S(2)}, u32[]{:S(2)}) %collective-permute-start.22) | collective-permute-done | bytes 589856 | tf_op jit(solution)/shard_map/ppermute | solution.py:699
  121.3 2.3 %collective-permute-done.24 = bf16[256,1536]{1,0:T(8,128)(2,1)S(1)} collective-permute-done((bf16[256,1536]{1,0:T(8,128)(2,1)S(1)}, bf16[256,1536]{1,0:T(8,128)(2,1)S(1)}, u32[]{:S(2)}, u32[]{:S(2)}) %collective-permute-start.24) | collective-permute-done | bytes 786464 | tf_op jit(solution)/shard_map/ppermute | solution.py:699
  123.7 1.7 %collective-permute-start.27 = (bf16[64,1536]{1,0:T(8,128)(2,1)S(1)}, bf16[64,1536]{1,0:T(8,128)(2,1)S(1)}, u32[]{:S(2)}, u32[]{:S(2)}) collective-permute-start(bf16[64,1536]{1,0:T(8,128)(2,1)S(1)} %get-tuple-element.144), channel_id=1, source_target_pairs={{0,6},{1,7},{2,4},{3,5},{4,2},{5,3},{6,0},{7,1},{8,14},{9,15},{10,... | collective-permute-start | bytes 589832 | tf_op jit(solution)/shard_map/ppermute | solution.py:699
  125.4 1.3 collective-permute-start.26
  127.3 1.7 %collective-permute-start.33 = (bf16[16,4608]{1,0:T(8,128)(2,1)S(1)}, bf16[16,4608]{1,0:T(8,128)(2,1)S(1)}, u32[]{:S(2)}, u32[]{:S(2)}) collective-permute-start(bf16[16,4608]{1,0:T(8,128)(2,1)S(1)} %get-tuple-element.140), channel_id=1, source_target_pairs={{0,24},{1,25},{2,26},{3,27},{4,28},{5,29},{6,30},{7,31},{8,16},{9,... | collective-permute-start | bytes 442376 | tf_op jit(solution)/shard_map/ppermute | solution.py:699
  129.0 4.7 %finish.1 = (f32[1024,512]{1,0:T(8,128)}, bf16[512,128]{1,0:T(8,128)(2,1)}) custom-call(bf16[1024,512]{1,0:T(8,128)(2,1)S(1)} %copy-done.1, f32[16,512]{1,0:T(8,128)S(1)} %get-tuple-element.80.vec, f32[1024,512]{1,0:T(8,128)S(1)} %copy-done, bf16[512,1536]{1,0:T(8,128)(2,1)S(1)} %get-tuple-element.113.w, f32[8,512]{1,0:T(8,128)S(1)} %get-tuple-element.114.feed_sums, ...), custom_call_target="tpu_custom_call" | custom-call | flops 1610612736 | bytes 4456448 | tf_op jit(solution)/shard_map/finish/pallas_call | solution.py:586
  133.7 4.4 %all-to-all-start = ((bf16[32,16,128]{2,1,0:T(8,128)(2,1)}), bf16[32,16,128]{2,1,0:T(8,128)(2,1)S(1)}, u32[]{:S(2)}, u32[]{:S(2)}) async-start(bf16[32,16,128]{2,1,0:T(8,128)(2,1)} %bitcast.2), calls=%async_computation | async-start | bytes 262144 | tf_op jit(solution)/shard_map/all_to_all | solution.py:810
  138.1 1.8 %collective-permute-start.31 = (bf16[16,4608]{1,0:T(8,128)(2,1)S(1)}, bf16[16,4608]{1,0:T(8,128)(2,1)S(1)}, u32[]{:S(2)}, u32[]{:S(2)}) collective-permute-start(bf16[16,4608]{1,0:T(8,128)(2,1)S(1)} %get-tuple-element.142), channel_id=1, source_target_pairs={{0,8},{1,9},{2,10},{3,11},{4,12},{5,13},{6,14},{7,15},{8,0},{9,1},... | collective-permute-start | bytes 442376 | tf_op jit(solution)/shard_map/ppermute | solution.py:699
  140.0 2.4 %collective-permute-start.30 = (bf16[16,1536]{1,0:T(8,128)(2,1)S(1)}, bf16[16,1536]{1,0:T(8,128)(2,1)S(1)}, u32[]{:S(2)}, u32[]{:S(2)}) collective-permute-start(bf16[16,1536]{1,0:T(8,128)(2,1)S(1)} %get-tuple-element.148), channel_id=1, source_target_pairs={{0,24},{1,25},{2,26},{3,27},{4,28},{5,29},{6,30},{7,31},{8,16},{9,... | collective-permute-start | bytes 147464 | tf_op jit(solution)/shard_map/ppermute | solution.py:699
  142.6 1.9 %collective-permute-start.28 = (bf16[16,1536]{1,0:T(8,128)(2,1)S(1)}, bf16[16,1536]{1,0:T(8,128)(2,1)S(1)}, u32[]{:S(2)}, u32[]{:S(2)}) collective-permute-start(bf16[16,1536]{1,0:T(8,128)(2,1)S(1)} %get-tuple-element.150), channel_id=1, source_target_pairs={{0,8},{1,9},{2,10},{3,11},{4,12},{5,13},{6,14},{7,15},{8,0},{9,1},... | collective-permute-start | bytes 147464 | tf_op jit(solution)/shard_map/ppermute | solution.py:699
  144.5 4.0 %collective-permute-done.31.refs_1_ = bf16[16,4608]{1,0:T(8,128)(2,1)S(1)} collective-permute-done((bf16[16,4608]{1,0:T(8,128)(2,1)S(1)}, bf16[16,4608]{1,0:T(8,128)(2,1)S(1)}, u32[]{:S(2)}, u32[]{:S(2)}) %collective-permute-start.31) | collective-permute-done | bytes 147488 | tf_op jit(solution)/shard_map/ppermute | solution.py:699
  150.7 1.5 collect.1
  (64 shorter events, 11.8 us)
Async XLA Ops:
  2.4 11.0 %collective-permute-start.2 = (bf16[16,1664]{1,0:T(8,128)(2,1)}, bf16[16,1664]{1,0:T(8,128)(2,1)S(1)}, u32[]{:S(2)}, u32[]{:S(2)}) collective-permute-start(bf16[16,1664]{1,0:T(8,128)(2,1)} %pack.1), channel_id=1, source_target_pairs={{0,24},{1,25},{2,26},{3,27},{4,28},{5,29},{6,30},{7,31},{8,16},{9,... | collective-permute-start | bytes 159752 | tf_op jit(solution)/shard_map/ppermute | solution.py:699
  7.5 6.0 %collective-permute-start.1 = (bf16[16,1664]{1,0:T(8,128)(2,1)}, bf16[16,1664]{1,0:T(8,128)(2,1)S(1)}, u32[]{:S(2)}, u32[]{:S(2)}) collective-permute-start(bf16[16,1664]{1,0:T(8,128)(2,1)} %pack.1), channel_id=1, source_target_pairs={{0,16},{1,17},{2,18},{3,19},{4,20},{5,21},{6,22},{7,23},{8,24},{9,... | collective-permute-start | bytes 159752 | tf_op jit(solution)/shard_map/ppermute | solution.py:699
  7.5 6.0 %collective-permute-start = (bf16[16,1664]{1,0:T(8,128)(2,1)}, bf16[16,1664]{1,0:T(8,128)(2,1)S(1)}, u32[]{:S(2)}, u32[]{:S(2)}) collective-permute-start(bf16[16,1664]{1,0:T(8,128)(2,1)} %pack.1), channel_id=1, source_target_pairs={{0,8},{1,9},{2,10},{3,11},{4,12},{5,13},{6,14},{7,15},{8,0},{9,1},... | collective-permute-start | bytes 159752 | tf_op jit(solution)/shard_map/ppermute | solution.py:699
  9.6 10.1 %collective-permute-start.12 = (bf16[16,4608]{1,0:T(8,128)(2,1)}, bf16[16,4608]{1,0:T(8,128)(2,1)S(1)}, u32[]{:S(2)}, u32[]{:S(2)}) collective-permute-start(bf16[16,4608]{1,0:T(8,128)(2,1)} %join.1), channel_id=1, source_target_pairs={{0,24},{1,25},{2,26},{3,27},{4,28},{5,29},{6,30},{7,31},{8,16},{9,... | collective-permute-start | bytes 442376 | tf_op jit(solution)/shard_map/ppermute | solution.py:699
  14.3 12.3 %collective-permute-start.5 = (bf16[64,1664]{1,0:T(8,128)(2,1)S(1)}, bf16[64,1664]{1,0:T(8,128)(2,1)S(1)}, u32[]{:S(2)}, u32[]{:S(2)}) collective-permute-start(bf16[64,1664]{1,0:T(8,128)(2,1)S(1)} %pad_maximum_fusion.refs_0_), channel_id=1, source_target_pairs={{0,6},{1,7},{2,4},{3,5},{4,2},{5,3},{6,0},{7,1},{8,14},{9,15},{10,... | collective-permute-start | bytes 638984 | tf_op jit(solution)/shard_map/ppermute | solution.py:699
  16.8 9.8 %collective-permute-start.4 = (bf16[64,1664]{1,0:T(8,128)(2,1)S(1)}, bf16[64,1664]{1,0:T(8,128)(2,1)S(1)}, u32[]{:S(2)}, u32[]{:S(2)}) collective-permute-start(bf16[64,1664]{1,0:T(8,128)(2,1)S(1)} %pad_maximum_fusion.refs_0_), channel_id=1, source_target_pairs={{0,4},{1,5},{2,6},{3,7},{4,0},{5,1},{6,2},{7,3},{8,12},{9,13},{10,... | collective-permute-start | bytes 638984 | tf_op jit(solution)/shard_map/ppermute | solution.py:699
  17.3 9.3 %collective-permute-start.3 = (bf16[64,1664]{1,0:T(8,128)(2,1)S(1)}, bf16[64,1664]{1,0:T(8,128)(2,1)S(1)}, u32[]{:S(2)}, u32[]{:S(2)}) collective-permute-start(bf16[64,1664]{1,0:T(8,128)(2,1)S(1)} %pad_maximum_fusion.refs_0_), channel_id=1, source_target_pairs={{0,2},{1,3},{2,0},{3,1},{4,6},{5,7},{6,4},{7,5},{8,10},{9,11},{10,... | collective-permute-start | bytes 638984 | tf_op jit(solution)/shard_map/ppermute | solution.py:699
  17.8 7.7 %collective-permute-start.11 = (bf16[16,4608]{1,0:T(8,128)(2,1)}, bf16[16,4608]{1,0:T(8,128)(2,1)S(1)}, u32[]{:S(2)}, u32[]{:S(2)}) collective-permute-start(bf16[16,4608]{1,0:T(8,128)(2,1)} %join.1), channel_id=1, source_target_pairs={{0,16},{1,17},{2,18},{3,19},{4,20},{5,21},{6,22},{7,23},{8,24},{9,... | collective-permute-start | bytes 442376 | tf_op jit(solution)/shard_map/ppermute | solution.py:699
  19.7 6.9 %collective-permute-start.10 = (bf16[16,4608]{1,0:T(8,128)(2,1)}, bf16[16,4608]{1,0:T(8,128)(2,1)S(1)}, u32[]{:S(2)}, u32[]{:S(2)}) collective-permute-start(bf16[16,4608]{1,0:T(8,128)(2,1)} %join.1), channel_id=1, source_target_pairs={{0,8},{1,9},{2,10},{3,11},{4,12},{5,13},{6,14},{7,15},{8,0},{9,1},... | collective-permute-start | bytes 442376 | tf_op jit(solution)/shard_map/ppermute | solution.py:699
  25.5 5.7 %collective-permute-start.6 = (bf16[64,1664]{1,0:T(8,128)(2,1)S(1)}, bf16[64,1664]{1,0:T(8,128)(2,1)S(1)}, u32[]{:S(2)}, u32[]{:S(2)}) collective-permute-start(bf16[64,1664]{1,0:T(8,128)(2,1)S(1)} %pad_maximum_fusion.refs_0_), channel_id=1, source_target_pairs={{0,1},{1,0},{2,3},{3,2},{4,5},{5,4},{6,7},{7,6},{8,9},{9,8},{10,11... | collective-permute-start | bytes 638984 | tf_op jit(solution)/shard_map/ppermute | solution.py:699
  27.6 3.7 %collective-permute-start.9 = (bf16[64,1664]{1,0:T(8,128)(2,1)S(1)}, bf16[64,1664]{1,0:T(8,128)(2,1)S(1)}, u32[]{:S(2)}, u32[]{:S(2)}) collective-permute-start(bf16[64,1664]{1,0:T(8,128)(2,1)S(1)} %collective-permute-done.5.refs_3_), channel_id=1, source_target_pairs={{0,1},{1,0},{2,3},{3,2},{4,5},{5,4},{6,7},{7,6},{8,9},{9,8},{10,11... | collective-permute-start | bytes 638984 | tf_op jit(solution)/shard_map/ppermute | solution.py:699
  27.7 21.2 %collective-permute-start.15 = (bf16[64,4608]{1,0:T(8,128)(2,1)S(1)}, bf16[64,4608]{1,0:T(8,128)(2,1)S(1)}, u32[]{:S(2)}, u32[]{:S(2)}) collective-permute-start(bf16[64,4608]{1,0:T(8,128)(2,1)S(1)} %constant_dynamic-update-slice_fusion.refs_0_), channel_id=1, source_target_pairs={{0,6},{1,7},{2,4},{3,5},{4,2},{5,3},{6,0},{7,1},{8,14},{9,15},{10,... | collective-permute-start | bytes 1769480 | tf_op jit(solution)/shard_map/ppermute | solution.py:699
  30.2 26.8 %collective-permute-start.14 = (bf16[64,4608]{1,0:T(8,128)(2,1)S(1)}, bf16[64,4608]{1,0:T(8,128)(2,1)S(1)}, u32[]{:S(2)}, u32[]{:S(2)}) collective-permute-start(bf16[64,4608]{1,0:T(8,128)(2,1)S(1)} %constant_dynamic-update-slice_fusion.refs_0_), channel_id=1, source_target_pairs={{0,4},{1,5},{2,6},{3,7},{4,0},{5,1},{6,2},{7,3},{8,12},{9,13},{10,... | collective-permute-start | bytes 1769480 | tf_op jit(solution)/shard_map/ppermute | solution.py:699
  30.7 26.4 %collective-permute-start.13 = (bf16[64,4608]{1,0:T(8,128)(2,1)S(1)}, bf16[64,4608]{1,0:T(8,128)(2,1)S(1)}, u32[]{:S(2)}, u32[]{:S(2)}) collective-permute-start(bf16[64,4608]{1,0:T(8,128)(2,1)S(1)} %constant_dynamic-update-slice_fusion.refs_0_), channel_id=1, source_target_pairs={{0,2},{1,3},{2,0},{3,1},{4,6},{5,7},{6,4},{7,5},{8,10},{9,11},{10,... | collective-permute-start | bytes 1769480 | tf_op jit(solution)/shard_map/ppermute | solution.py:699
  32.7 24.9 %collective-permute-start.16 = (bf16[64,4608]{1,0:T(8,128)(2,1)S(1)}, bf16[64,4608]{1,0:T(8,128)(2,1)S(1)}, u32[]{:S(2)}, u32[]{:S(2)}) collective-permute-start(bf16[64,4608]{1,0:T(8,128)(2,1)S(1)} %constant_dynamic-update-slice_fusion.refs_0_), channel_id=1, source_target_pairs={{0,1},{1,0},{2,3},{3,2},{4,5},{5,4},{6,7},{7,6},{8,9},{9,8},{10,11... | collective-permute-start | bytes 1769480 | tf_op jit(solution)/shard_map/ppermute | solution.py:699
  57.1 2.8 %collective-permute-start.18 = (bf16[64,4608]{1,0:T(8,128)(2,1)S(1)}, bf16[64,4608]{1,0:T(8,128)(2,1)S(1)}, u32[]{:S(2)}, u32[]{:S(2)}) collective-permute-start(bf16[64,4608]{1,0:T(8,128)(2,1)S(1)} %collective-permute-done.14.refs_2_), channel_id=1, source_target_pairs={{0,1},{1,0},{2,3},{3,2},{4,5},{5,4},{6,7},{7,6},{8,9},{9,8},{10,11... | collective-permute-start | bytes 1769480 | tf_op jit(solution)/shard_map/ppermute | solution.py:699
  57.6 3.2 %collective-permute-start.19 = (bf16[64,4608]{1,0:T(8,128)(2,1)S(1)}, bf16[64,4608]{1,0:T(8,128)(2,1)S(1)}, u32[]{:S(2)}, u32[]{:S(2)}) collective-permute-start(bf16[64,4608]{1,0:T(8,128)(2,1)S(1)} %collective-permute-done.15.refs_3_), channel_id=1, source_target_pairs={{0,1},{1,0},{2,3},{3,2},{4,5},{5,4},{6,7},{7,6},{8,9},{9,8},{10,11... | collective-permute-start | bytes 1769480 | tf_op jit(solution)/shard_map/ppermute | solution.py:699
  83.8 7.2 %collective-permute-start.20 = (bf16[256,4608]{1,0:T(8,128)(2,1)}, bf16[256,4608]{1,0:T(8,128)(2,1)S(1)}, u32[]{:S(2)}, u32[]{:S(2)}) collective-permute-start(bf16[256,4608]{1,0:T(8,128)(2,1)} %get-tuple-element.93), channel_id=1, source_target_pairs={{0,1},{1,0},{2,3},{3,2},{4,5},{5,4},{6,7},{7,6},{8,9},{9,8},{10,11... | collective-permute-start | bytes 7077896 | tf_op jit(solution)/shard_map/ppermute | solution.py:699
  91.6 25.6 %collective-permute-start.23 = (bf16[64,4608]{1,0:T(8,128)(2,1)S(1)}, bf16[64,4608]{1,0:T(8,128)(2,1)S(1)}, u32[]{:S(2)}, u32[]{:S(2)}) collective-permute-start(bf16[64,4608]{1,0:T(8,128)(2,1)S(1)} %get-tuple-element.136), channel_id=1, source_target_pairs={{0,6},{1,7},{2,4},{3,5},{4,2},{5,3},{6,0},{7,1},{8,14},{9,15},{10,... | collective-permute-start | bytes 1769480 | tf_op jit(solution)/shard_map/ppermute | solution.py:699
  93.3 27.5 %collective-permute-start.22 = (bf16[64,4608]{1,0:T(8,128)(2,1)S(1)}, bf16[64,4608]{1,0:T(8,128)(2,1)S(1)}, u32[]{:S(2)}, u32[]{:S(2)}) collective-permute-start(bf16[64,4608]{1,0:T(8,128)(2,1)S(1)} %get-tuple-element.137), channel_id=1, source_target_pairs={{0,4},{1,5},{2,6},{3,7},{4,0},{5,1},{6,2},{7,3},{8,12},{9,13},{10,... | collective-permute-start | bytes 1769480 | tf_op jit(solution)/shard_map/ppermute | solution.py:699
  94.7 26.2 %collective-permute-start.21 = (bf16[64,4608]{1,0:T(8,128)(2,1)S(1)}, bf16[64,4608]{1,0:T(8,128)(2,1)S(1)}, u32[]{:S(2)}, u32[]{:S(2)}) collective-permute-start(bf16[64,4608]{1,0:T(8,128)(2,1)S(1)} %get-tuple-element.138), channel_id=1, source_target_pairs={{0,2},{1,3},{2,0},{3,1},{4,6},{5,7},{6,4},{7,5},{8,10},{9,11},{10,... | collective-permute-start | bytes 1769480 | tf_op jit(solution)/shard_map/ppermute | solution.py:699
  121.2 2.4 %collective-permute-start.24 = (bf16[256,1536]{1,0:T(8,128)(2,1)S(1)}, bf16[256,1536]{1,0:T(8,128)(2,1)S(1)}, u32[]{:S(2)}, u32[]{:S(2)}) collective-permute-start(bf16[256,1536]{1,0:T(8,128)(2,1)S(1)} %get-tuple-element.111), channel_id=1, source_target_pairs={{0,1},{1,0},{2,3},{3,2},{4,5},{5,4},{6,7},{7,6},{8,9},{9,8},{10,11... | collective-permute-start | bytes 2359304 | tf_op jit(solution)/shard_map/ppermute | solution.py:699
  123.7 14.3 %collective-permute-start.27 = (bf16[64,1536]{1,0:T(8,128)(2,1)S(1)}, bf16[64,1536]{1,0:T(8,128)(2,1)S(1)}, u32[]{:S(2)}, u32[]{:S(2)}) collective-permute-start(bf16[64,1536]{1,0:T(8,128)(2,1)S(1)} %get-tuple-element.144), channel_id=1, source_target_pairs={{0,6},{1,7},{2,4},{3,5},{4,2},{5,3},{6,0},{7,1},{8,14},{9,15},{10,... | collective-permute-start | bytes 589832 | tf_op jit(solution)/shard_map/ppermute | solution.py:699
  125.4 14.5 %collective-permute-start.26 = (bf16[64,1536]{1,0:T(8,128)(2,1)S(1)}, bf16[64,1536]{1,0:T(8,128)(2,1)S(1)}, u32[]{:S(2)}, u32[]{:S(2)}) collective-permute-start(bf16[64,1536]{1,0:T(8,128)(2,1)S(1)} %get-tuple-element.145), channel_id=1, source_target_pairs={{0,4},{1,5},{2,6},{3,7},{4,0},{5,1},{6,2},{7,3},{8,12},{9,13},{10,... | collective-permute-start | bytes 589832 | tf_op jit(solution)/shard_map/ppermute | solution.py:699
  126.7 13.2 %collective-permute-start.25 = (bf16[64,1536]{1,0:T(8,128)(2,1)S(1)}, bf16[64,1536]{1,0:T(8,128)(2,1)S(1)}, u32[]{:S(2)}, u32[]{:S(2)}) collective-permute-start(bf16[64,1536]{1,0:T(8,128)(2,1)S(1)} %get-tuple-element.146), channel_id=1, source_target_pairs={{0,2},{1,3},{2,0},{3,1},{4,6},{5,7},{6,4},{7,5},{8,10},{9,11},{10,... | collective-permute-start | bytes 589832 | tf_op jit(solution)/shard_map/ppermute | solution.py:699
  127.3 15.3 %collective-permute-start.33 = (bf16[16,4608]{1,0:T(8,128)(2,1)S(1)}, bf16[16,4608]{1,0:T(8,128)(2,1)S(1)}, u32[]{:S(2)}, u32[]{:S(2)}) collective-permute-start(bf16[16,4608]{1,0:T(8,128)(2,1)S(1)} %get-tuple-element.140), channel_id=1, source_target_pairs={{0,24},{1,25},{2,26},{3,27},{4,28},{5,29},{6,30},{7,31},{8,16},{9,... | collective-permute-start | bytes 442376 | tf_op jit(solution)/shard_map/ppermute | solution.py:699
  129.0 15.5 %collective-permute-start.32 = (bf16[16,4608]{1,0:T(8,128)(2,1)S(1)}, bf16[16,4608]{1,0:T(8,128)(2,1)S(1)}, u32[]{:S(2)}, u32[]{:S(2)}) collective-permute-start(bf16[16,4608]{1,0:T(8,128)(2,1)S(1)} %get-tuple-element.141), channel_id=1, source_target_pairs={{0,16},{1,17},{2,18},{3,19},{4,20},{5,21},{6,22},{7,23},{8,24},{9,... | collective-permute-start | bytes 442376 | tf_op jit(solution)/shard_map/ppermute | solution.py:699
  133.7 17.0 %all-to-all-start = ((bf16[32,16,128]{2,1,0:T(8,128)(2,1)}), bf16[32,16,128]{2,1,0:T(8,128)(2,1)S(1)}, u32[]{:S(2)}, u32[]{:S(2)}) async-start(bf16[32,16,128]{2,1,0:T(8,128)(2,1)} %bitcast.2), calls=%async_computation | async-start | bytes 262144 | tf_op jit(solution)/shard_map/all_to_all | solution.py:810
  138.1 10.4 %collective-permute-start.31 = (bf16[16,4608]{1,0:T(8,128)(2,1)S(1)}, bf16[16,4608]{1,0:T(8,128)(2,1)S(1)}, u32[]{:S(2)}, u32[]{:S(2)}) collective-permute-start(bf16[16,4608]{1,0:T(8,128)(2,1)S(1)} %get-tuple-element.142), channel_id=1, source_target_pairs={{0,8},{1,9},{2,10},{3,11},{4,12},{5,13},{6,14},{7,15},{8,0},{9,1},... | collective-permute-start | bytes 442376 | tf_op jit(solution)/shard_map/ppermute | solution.py:699
  140.0 9.6 %collective-permute-start.30 = (bf16[16,1536]{1,0:T(8,128)(2,1)S(1)}, bf16[16,1536]{1,0:T(8,128)(2,1)S(1)}, u32[]{:S(2)}, u32[]{:S(2)}) collective-permute-start(bf16[16,1536]{1,0:T(8,128)(2,1)S(1)} %get-tuple-element.148), channel_id=1, source_target_pairs={{0,24},{1,25},{2,26},{3,27},{4,28},{5,29},{6,30},{7,31},{8,16},{9,... | collective-permute-start | bytes 147464 | tf_op jit(solution)/shard_map/ppermute | solution.py:699
  142.4 7.2 %collective-permute-start.29 = (bf16[16,1536]{1,0:T(8,128)(2,1)S(1)}, bf16[16,1536]{1,0:T(8,128)(2,1)S(1)}, u32[]{:S(2)}, u32[]{:S(2)}) collective-permute-start(bf16[16,1536]{1,0:T(8,128)(2,1)S(1)} %get-tuple-element.149), channel_id=1, source_target_pairs={{0,16},{1,17},{2,18},{3,19},{4,20},{5,21},{6,22},{7,23},{8,24},{9,... | collective-permute-start | bytes 147464 | tf_op jit(solution)/shard_map/ppermute | solution.py:699
  142.6 7.4 %collective-permute-start.28 = (bf16[16,1536]{1,0:T(8,128)(2,1)S(1)}, bf16[16,1536]{1,0:T(8,128)(2,1)S(1)}, u32[]{:S(2)}, u32[]{:S(2)}) collective-permute-start(bf16[16,1536]{1,0:T(8,128)(2,1)S(1)} %get-tuple-element.150), channel_id=1, source_target_pairs={{0,8},{1,9},{2,10},{3,11},{4,12},{5,13},{6,14},{7,15},{8,0},{9,1},... | collective-permute-start | bytes 147464 | tf_op jit(solution)/shard_map/ppermute | solution.py:699
  (6 other events, 52.5 us)
